TPU v7x, 256 devices: a whole 4x4x8 slice. The times are simulated.
256 devices in a mesh: gx: 32 (over y, z_lo, core), gy: 8 (over z_hi, x).
Axes of the slice: x: 4, y: 4, z: 8 (z_hi: 2, z_lo: 4; z = z_hi * 4 + z_lo), core: 2. Of those that a mesh axis runs over, the one named last changes fastest.
Arguments:
- tokens: bfloat16 [256, 64, 6144], P('gx', 'gy'), may hold values from -6 to 6
- upstream: bfloat16 [256, 64, 6144], P('gx', 'gy'), may hold values from -16 to 16
- gain_one: float32 [96], replicated, may hold values from 0.1 to 1.9
- gain_two: float32 [96], replicated, may hold values from 0.1 to 1.9
- attn_weight: bfloat16 [96, 288], replicated, may hold values from -2 to 2
- proj_weight: bfloat16 [96, 96], replicated, may hold values from -0.625 to 0.625
- expand_weight: bfloat16 [96, 384], replicated, may hold values from -0.625 to 0.625
- reduce_weight: bfloat16 [384, 96], replicated, may hold values from -0.3125 to 0.3125
Outputs:
- grad_tokens: bfloat16 [256, 64, 6144], P('gx', 'gy')
- grad_gain_one: float32 [96], replicated
- grad_gain_two: float32 [96], replicated
- grad_attn: float32 [96, 288], replicated
- grad_proj: float32 [96, 96], replicated
- grad_expand: float32 [96, 384], replicated
- grad_reduce: float32 [384, 96], replicated
All inputs are finite; a program needn't handle non-finite values.
Results may differ from a plain program's by a relative error of at most 0.023.
The roundings to bfloat16 on the way count: a program that leaves them out, or rounds other values in their place, can miss the bound.
Values may be sent and summed in bfloat16 or wider, within the bound.
A program may use at most 128 MiB of HBM per device.

v0:
```python
import math

import jax
import jax.numpy as jnp
from jax import lax
from jax.sharding import PartitionSpec as P

D = 96
HEADS = 3
WIN = 8


epsilon = 1e-05


def shifted(value, axis, steps):
    count = lax.axis_size(axis)
    pairs = [(source, (source + steps) % count) for source in range(count)]
    return lax.ppermute(value, axis, pairs)


def norm_rows(row_data, gain_vec):
    centre = row_data - jnp.mean(row_data, axis=-1, keepdims=True)
    inverse = lax.rsqrt(jnp.mean(centre * centre, axis=-1, keepdims=True) + epsilon)
    normed = centre * inverse
    return (normed * gain_vec, normed, inverse)


def norm_back(grad_out, normed, inverse, gain_vec):
    scaled = grad_out * gain_vec
    mean_one = jnp.mean(scaled, axis=-1, keepdims=True)
    mean_two = jnp.mean(scaled * normed, axis=-1, keepdims=True)
    return (inverse * (scaled - mean_one - normed * mean_two), jnp.sum(grad_out * normed, axis=0))


def to_windows(grid_four):
    ext_x, ext_y, ext_z, width = grid_four.shape
    split = grid_four.reshape(ext_x // WIN, WIN, ext_y // WIN, WIN, ext_z // WIN, WIN, width)
    return split.transpose(0, 2, 4, 1, 3, 5, 6).reshape(-1, WIN**3, width)


def from_windows(windows, ext_x, ext_y, ext_z):
    width = windows.shape[-1]
    split = windows.reshape(ext_x // WIN, ext_y // WIN, ext_z // WIN, WIN, WIN, WIN, width)
    return split.transpose(0, 3, 1, 4, 2, 5, 6).reshape(ext_x, ext_y, ext_z, width)


def split_heads(packed):
    length = packed.shape[0]
    return packed.reshape(length, 3, HEADS, D // HEADS).transpose(1, 2, 0, 3)


def attend(packed):
    length = packed.shape[0]
    factor = (D // HEADS) ** (-0.5)
    parts = split_heads(packed)
    scores = (
        jnp.einsum("hqd,hkd->hqk", parts[0], parts[1], preferred_element_type=jnp.float32) * factor
    )
    weights = jnp.exp(scores - jnp.max(scores, axis=-1, keepdims=True))
    probs = (weights / jnp.sum(weights, axis=-1, keepdims=True)).astype(jnp.bfloat16)
    mixed = jnp.einsum("hqk,hkd->hqd", probs, parts[2], preferred_element_type=jnp.float32).astype(
        jnp.bfloat16
    )
    return (mixed.transpose(1, 0, 2).reshape(length, D), probs)


def attend_back(items):
    packed, probs, grad_mix = items
    length = packed.shape[0]
    factor = (D // HEADS) ** (-0.5)
    parts = split_heads(packed)
    grad_heads = grad_mix.reshape(length, HEADS, D // HEADS).transpose(1, 0, 2)
    grad_probs = jnp.einsum(
        "hqd,hkd->hqk", grad_heads, parts[2], preferred_element_type=jnp.float32
    )
    grad_values = jnp.einsum("hqk,hqd->hkd", probs, grad_heads, preferred_element_type=jnp.float32)
    probs_wide = probs.astype(jnp.float32)
    grad_scores = (
        probs_wide
        * (grad_probs - jnp.sum(grad_probs * probs_wide, axis=-1, keepdims=True))
        * factor
    )
    grad_scores = grad_scores.astype(jnp.bfloat16)
    grad_queries = jnp.einsum(
        "hqk,hkd->hqd", grad_scores, parts[1], preferred_element_type=jnp.float32
    )
    grad_keys = jnp.einsum(
        "hqk,hqd->hkd", grad_scores, parts[0], preferred_element_type=jnp.float32
    )
    stacked = jnp.stack([grad_queries, grad_keys, grad_values])
    return stacked.transpose(2, 0, 1, 3).reshape(length, 3 * D).astype(jnp.bfloat16)


def mlp_back(resid_rows, grad_rows, gain_two, expand_weight, reduce_weight):
    resid = resid_rows.astype(jnp.float32)
    h2f, normed, inverse = norm_rows(resid, gain_two)
    h2 = h2f.astype(jnp.bfloat16)
    pre_act = jnp.dot(h2, expand_weight, preferred_element_type=jnp.float32)
    act, gelu_back = jax.vjp(jax.nn.gelu, pre_act)
    act_b = act.astype(jnp.bfloat16)
    sum_reduce = jnp.dot(act_b.T, grad_rows, preferred_element_type=jnp.float32)
    grad_act = jnp.dot(grad_rows, reduce_weight.T, preferred_element_type=jnp.float32)
    grad_pre = gelu_back(grad_act)[0].astype(jnp.bfloat16)
    sum_expand = jnp.dot(h2.T, grad_pre, preferred_element_type=jnp.float32)
    grad_h2 = jnp.dot(grad_pre, expand_weight.T, preferred_element_type=jnp.float32)
    part_grad, sum_two = norm_back(grad_h2, normed, inverse, gain_two)
    return (grad_rows.astype(jnp.float32) + part_grad, sum_expand, sum_reduce, sum_two)


def ahead(slab_in):
    half_win = WIN // 2
    moved = shifted(slab_in[:half_win], "gx", -1)
    slab_in = jnp.concatenate([slab_in[half_win:], moved], axis=0)
    moved = shifted(slab_in[:, :half_win], "gy", -1)
    slab_in = jnp.concatenate([slab_in[:, half_win:], moved], axis=1)
    return jnp.roll(slab_in, -half_win * D, axis=2)


def behind(slab_in):
    half_win = WIN // 2
    slab_in = jnp.roll(slab_in, half_win * D, axis=2)
    moved = shifted(slab_in[:, -half_win:], "gy", 1)
    slab_in = jnp.concatenate([moved, slab_in[:, :-half_win]], axis=1)
    moved = shifted(slab_in[-half_win:], "gx", 1)
    return jnp.concatenate([moved, slab_in[:-half_win]], axis=0)


def local(
    tokens, upstream, gain_one, gain_two, attn_weight, proj_weight, expand_weight, reduce_weight
):
    rows_x, rows_y, merged = tokens.shape
    depth = merged // D
    count_all = rows_x * rows_y * depth * lax.axis_size("gx") * lax.axis_size("gy")
    factor = 1.0 / math.sqrt(count_all)
    base = tokens.reshape(-1, D).astype(jnp.float32)
    h1f, normed_one, inverse_one = norm_rows(base, gain_one)
    h1 = h1f.astype(jnp.bfloat16)
    rolled_flat = ahead(h1.reshape(rows_x, rows_y, merged)).reshape(-1, D)
    packed = jnp.dot(rolled_flat, attn_weight, preferred_element_type=jnp.float32).astype(
        jnp.bfloat16
    )
    packed_win = to_windows(packed.reshape(rows_x, rows_y, depth, 3 * D))
    mixed_win, probs_win = lax.map(attend, packed_win)
    mixed = from_windows(mixed_win, rows_x, rows_y, depth).reshape(-1, D)
    branch = jnp.dot(mixed, proj_weight, preferred_element_type=jnp.float32).astype(jnp.bfloat16)
    branch_back = behind(branch.reshape(rows_x, rows_y, merged)).reshape(-1, D)
    resid = (base + branch_back.astype(jnp.float32)).astype(jnp.bfloat16)
    grad_resid, sum_expand, sum_reduce, sum_two = mlp_back(
        resid, upstream.reshape(-1, D), gain_two, expand_weight, reduce_weight
    )
    grad_branch = grad_resid.astype(jnp.bfloat16)
    grad_branch = ahead(grad_branch.reshape(rows_x, rows_y, merged)).reshape(-1, D)
    sum_proj = jnp.dot(mixed.T, grad_branch, preferred_element_type=jnp.float32)
    grad_mix = jnp.dot(grad_branch, proj_weight.T, preferred_element_type=jnp.float32).astype(
        jnp.bfloat16
    )
    grad_mix_win = to_windows(grad_mix.reshape(rows_x, rows_y, depth, D))
    grad_packed_win = lax.map(attend_back, (packed_win, probs_win, grad_mix_win))
    grad_packed = from_windows(grad_packed_win, rows_x, rows_y, depth).reshape(-1, 3 * D)
    sum_attn = jnp.dot(rolled_flat.T, grad_packed, preferred_element_type=jnp.float32)
    grad_in = jnp.dot(grad_packed, attn_weight.T, preferred_element_type=jnp.float32).astype(
        jnp.bfloat16
    )
    grad_h1 = behind(grad_in.reshape(rows_x, rows_y, merged)).reshape(-1, D)
    part_grad, sum_one = norm_back(grad_h1.astype(jnp.float32), normed_one, inverse_one, gain_one)
    grad_tokens = (grad_resid + part_grad).astype(jnp.bfloat16).reshape(rows_x, rows_y, merged)
    sum_attn, sum_proj, sum_expand, sum_reduce, sum_one, sum_two = lax.psum(
        (sum_attn, sum_proj, sum_expand, sum_reduce, sum_one, sum_two), ("gx", "gy")
    )
    return (
        grad_tokens,
        sum_one * factor,
        sum_two * factor,
        sum_attn * factor,
        sum_proj * factor,
        sum_expand * factor,
        sum_reduce * factor,
    )


def solution(mesh):
    return jax.shard_map(
        local,
        mesh=mesh,
        in_specs=(P("gx", "gy", None), P("gx", "gy", None), P(), P(), P(), P(), P(), P()),
        out_specs=(P("gx", "gy", None), P(), P(), P(), P(), P(), P()),
        check_vma=False,
    )
```

profile of v0, /device:TPU:1, one launch (start us, length us, event | category | flops | bytes accessed | tf_op | source)
XLA Modules:
  0.0 667.3 jit_solution(129284855867884805)
XLA Ops:
  7.2 3.0 reshape.140
  10.2 1.9 copy.35
  12.1 2.8 reduce_sum.108
  16.8 3.3 collective-permute-start
  21.1 4.2 collective-permute-done
  25.7 8.9 %collective-permute-start.1 = (bf16[8,4,6144]{2,1,0:T(4,128)(2,1)S(1)}, bf16[8,4,6144]{2,1,0:T(4,128)(2,1)S(1)}, u32[]{:S(2)}, u32[]{:S(2)}) collective-permute-start(bf16[8,4,6144]{2,1,0:T(4,128)(2,1)S(1)} %get-tuple-element.114), channel_id=1, source_target_pairs={{0,7},{1,0},{2,1},{3,2},{4,3},{5,4},{6,5},{7,6},{8,15},{9,8},{10,9... | collective-permute-start | bytes 1179656 | tf_op jit(solution)/shard_map/ppermute | solution.py:19
  34.6 8.1 %collective-permute-done.1 = bf16[8,4,6144]{2,1,0:T(4,128)(2,1)S(1)} collective-permute-done((bf16[8,4,6144]{2,1,0:T(4,128)(2,1)S(1)}, bf16[8,4,6144]{2,1,0:T(4,128)(2,1)S(1)}, u32[]{:S(2)}, u32[]{:S(2)}) %collective-permute-start.1) | collective-permute-done | bytes 393248 | tf_op jit(solution)/shard_map/ppermute | solution.py:19
  45.2 2.2 convolution_convert_fusion.1
  47.4 3.3 copy.29
  50.7 2.2 copy.30
  52.9 4.5 copy.31
  57.4 38.9 %while.22 = (s32[]{:T(128)}, bf16[8,512,96]{1,2,0:T(8,128)(2,1)}, bf16[8,3,512,512]{2,3,1,0:T(8,128)(2,1)}, bf16[8,512,288]{1,2,0:T(8,128)(2,1)}, s32[]{:T(128)}) while((s32[]{:T(128)}, bf16[8,512,96]{1,2,0:T(8,128)(2,1)}, bf16[8,3,512,512]{2,3,1,0:T(8,128)(2,1)}, bf16[8,512,288]{1,2,0:T(8,128)(2,1)}, s32[]{:T(128)}) %tuple.56), condition=%wide.region_5.6_spmd, body=%wide.region_2.5_spmd.sunk | while | flops 104645120 | bytes 12203073 | solution.py:144
  69.3 1.6 bitcast_dynamic-update-slice_fusion.4
  74.1 1.6 bitcast_dynamic-update-slice_fusion.4
  83.8 1.7 bitcast_dynamic-update-slice_fusion.4
  93.6 1.6 bitcast_dynamic-update-slice_fusion.4
  102.2 13.4 %collective-permute-done.2 = bf16[8,4,6144]{2,1,0:T(4,128)(2,1)S(1)} collective-permute-done((bf16[8,4,6144]{2,1,0:T(4,128)(2,1)S(1)}, bf16[8,4,6144]{2,1,0:T(4,128)(2,1)S(1)}, u32[]{:S(2)}, u32[]{:S(2)}) %collective-permute-start.2) | collective-permute-done | bytes 393248 | tf_op jit(solution)/shard_map/ppermute | solution.py:19
  116.7 15.2 %collective-permute-start.3 = (bf16[4,8,6144]{2,1,0:T(8,128)(2,1)}, bf16[4,8,6144]{2,1,0:T(8,128)(2,1)S(1)}, u32[]{:S(2)}, u32[]{:S(2)}) collective-permute-start(bf16[4,8,6144]{2,1,0:T(8,128)(2,1)} %get-tuple-element.111), channel_id=1, source_target_pairs={{0,8},{8,16},{16,24},{24,32},{32,40},{40,48},{48,56},{56,64},{64,7... | collective-permute-start | bytes 1179656 | tf_op jit(solution)/shard_map/ppermute | solution.py:19
  133.4 3.5 collective-permute-done.3
  138.7 2.1 reshape.141
  140.9 2.9 copy.36
  143.8 1.7 convert_reduce_fusion
  147.1 4.9 fusion.54
  152.0 1.8 fusion.67
  157.1 9.2 %collective-permute-start.4 = (bf16[4,8,6144]{2,1,0:T(8,128)(2,1)S(1)}, bf16[4,8,6144]{2,1,0:T(8,128)(2,1)S(1)}, u32[]{:S(2)}, u32[]{:S(2)}) collective-permute-start(bf16[4,8,6144]{2,1,0:T(8,128)(2,1)S(1)} %slice.123), channel_id=1, source_target_pairs={{0,248},{8,0},{16,8},{24,16},{32,24},{40,32},{48,40},{56,48},{64,5... | collective-permute-start | bytes 1179656 | tf_op jit(solution)/shard_map/ppermute | solution.py:19
  168.5 5.3 fusion.55
  175.2 8.6 %collective-permute-done.5 = bf16[8,4,6144]{2,1,0:T(4,128)(2,1)S(1)} collective-permute-done((bf16[8,4,6144]{2,1,0:T(4,128)(2,1)S(1)}, bf16[8,4,6144]{2,1,0:T(4,128)(2,1)S(1)}, u32[]{:S(2)}, u32[]{:S(2)}) %collective-permute-start.5) | collective-permute-done | bytes 393248 | tf_op jit(solution)/shard_map/ppermute | solution.py:19
  187.2 88.0 %while.23 = (s32[]{:T(128)}, bf16[8,512,288]{1,2,0:T(8,128)(2,1)}, bf16[8,3,512,512]{2,3,1,0:T(8,128)(2,1)}, bf16[8,512,96]{1,2,0:T(8,128)(2,1)S(1)}, bf16[8,512,288]{1,2,0:T(8,128)(2,1)}, /*index=5*/s32[]{:T(128)}) while((s32[]{:T(128)}, bf16[8,512,288]{1,2,0:T(8,128)(2,1)}, bf16[8,3,512,512]{2,3,1,0:T(8,128)(2,1)}, ...), condition=%wide.region_12.13_spmd, body=%wide.region_10.12_spmd.sunk | while | flops 212783104 | bytes 33819808 | solution.py:159
  189.2 3.2 fusion.134
  192.4 3.1 fusion.133
  195.5 2.0 fusion.131
  200.2 3.1 fusion.134
  203.4 3.0 fusion.133
  206.4 2.0 fusion.131
  211.1 3.2 fusion.134
  214.3 3.1 fusion.133
  217.4 2.0 fusion.131
  222.1 3.1 fusion.134
  225.3 3.1 fusion.133
  228.3 2.0 fusion.131
  233.1 3.2 fusion.134
  236.3 3.1 fusion.133
  239.4 2.0 fusion.131
  244.1 3.2 fusion.134
  247.3 3.1 fusion.133
  250.4 2.0 fusion.131
  255.1 3.2 fusion.134
  258.3 3.1 fusion.133
  261.4 2.0 fusion.131
  266.1 3.1 fusion.134
  269.3 3.1 fusion.133
  272.4 2.0 fusion.131
  275.2 4.5 copy.43
  279.7 2.5 copy.44
  283.7 2.0 convolution_convert_fusion.2
  287.2 2.4 reshape.138
  292.7 262.4 %all-reduce.4.cloned.1.call-done = (f32[96,288]{1,0:T(8,128)}, f32[96,384]{1,0:T(8,128)}, f32[384,96]{0,1:T(8,128)}) async-done(((f32[96,288]{1,0:T(8,128)}, f32[96,384]{1,0:T(8,128)}, f32[384,96]{0,1:T(8,128)}), (f32[96,288]{1,0:T(8,128)}, f32[96,384]{1,0:T(8,128)}, f32[384,96]{0,1:T(8,128)})) %all-reduce.4.cloned.1.call-update) | async-done | bytes 405520 | tf_op jit(solution)/shard_map/psum | solution.py:168
  560.3 3.4 collective-permute-done.7
  563.8 2.2 reshape.142
  566.0 2.9 copy.46
  568.9 2.1 multiply_reduce_fusion.1
  571.1 79.7 %all-reduce = (f32[96]{0:T(128)S(1)}, f32[96]{0:T(128)S(1)}, f32[96,96]{1,0:T(8,128)S(1)}) all-reduce(f32[96]{0:T(128)S(1)} %get-tuple-element.69, f32[96]{0:T(128)S(1)} %copy-done.40, f32[96,96]{1,0:T(8,128)S(1)} %fusion.94), channel_id=1, replica_groups=mesh['gx'=32,'gy'=8] {'gx','gy'}, use_global_device_ids=true, to_apply=%region_16.17 | all-reduce | flops 9408 | bytes 75264 | tf_op jit(solution)/shard_map/psum | solution.py:168
  652.5 3.9 add_convert_fusion
  657.9 2.4 reshape.139
  (285 shorter events, 96.0 us)
Async XLA Ops:
  7.2 138.7 %copy-start = (bf16[96,384]{1,0:T(8,128)(2,1)S(1)}, bf16[96,384]{1,0:T(8,128)(2,1)}, u32[]{:S(2)}) copy-start(bf16[96,384]{1,0:T(8,128)(2,1)} %param.18) | copy-start | bytes 221188
  7.2 547.9 %all-reduce.4.cloned.1.call-start = ((), (), s32[]{:S(2)}) async-start(), calls=%async_computation | async-start | bytes 884736 | tf_op jit(solution)/shard_map/psum | solution.py:168
  12.1 3.0 copy-start.2
  12.1 3.0 copy-start.39
  16.8 8.6 %collective-permute-start = (bf16[4,8,6144]{2,1,0:T(8,128)(2,1)S(1)}, bf16[4,8,6144]{2,1,0:T(8,128)(2,1)S(1)}, u32[]{:S(2)}, u32[]{:S(2)}) collective-permute-start(bf16[4,8,6144]{2,1,0:T(8,128)(2,1)S(1)} %slice.109), channel_id=1, source_target_pairs={{0,248},{8,0},{16,8},{24,16},{32,24},{40,32},{48,40},{56,48},{64,5... | collective-permute-start | bytes 1179656 | tf_op jit(solution)/shard_map/ppermute | solution.py:19
  25.7 17.0 %collective-permute-start.1 = (bf16[8,4,6144]{2,1,0:T(4,128)(2,1)S(1)}, bf16[8,4,6144]{2,1,0:T(4,128)(2,1)S(1)}, u32[]{:S(2)}, u32[]{:S(2)}) collective-permute-start(bf16[8,4,6144]{2,1,0:T(4,128)(2,1)S(1)} %get-tuple-element.114), channel_id=1, source_target_pairs={{0,7},{1,0},{2,1},{3,2},{4,3},{5,4},{6,5},{7,6},{8,15},{9,8},{10,9... | collective-permute-start | bytes 1179656 | tf_op jit(solution)/shard_map/ppermute | solution.py:19
  43.1 2.1 copy-start.27
  44.2 1.0 copy-start.13
  96.3 2.8 copy-start.37
  98.1 1.0 copy-start.9
  102.1 29.8 %copy-start.23 = (bf16[8,8,6144]{2,1,0:T(8,128)(2,1)S(1)}, bf16[8,8,6144]{2,1,0:T(8,128)(2,1)}, u32[]{:S(2)}) copy-start(bf16[8,8,6144]{2,1,0:T(8,128)(2,1)} %param.13) | copy-start | bytes 2359300
  102.1 13.5 %collective-permute-start.2 = (bf16[8,4,6144]{2,1,0:T(4,128)(2,1)S(1)}, bf16[8,4,6144]{2,1,0:T(4,128)(2,1)S(1)}, u32[]{:S(2)}, u32[]{:S(2)}) collective-permute-start(bf16[8,4,6144]{2,1,0:T(4,128)(2,1)S(1)} %fusion.76), channel_id=1, source_target_pairs={{0,1},{1,2},{2,3},{3,4},{4,5},{5,6},{6,7},{7,0},{8,9},{9,10},{10,1... | collective-permute-start | bytes 1179656 | tf_op jit(solution)/shard_map/ppermute | solution.py:19
  116.7 20.2 %collective-permute-start.3 = (bf16[4,8,6144]{2,1,0:T(8,128)(2,1)}, bf16[4,8,6144]{2,1,0:T(8,128)(2,1)S(1)}, u32[]{:S(2)}, u32[]{:S(2)}) collective-permute-start(bf16[4,8,6144]{2,1,0:T(8,128)(2,1)} %get-tuple-element.111), channel_id=1, source_target_pairs={{0,8},{8,16},{16,24},{24,32},{32,40},{40,48},{48,56},{56,64},{64,7... | collective-permute-start | bytes 1179656 | tf_op jit(solution)/shard_map/ppermute | solution.py:19
  132.9 4.0 copy-start.18
  133.4 20.4 %copy-start.15 = (bf16[4096,96]{0,1:T(8,128)(2,1)}, bf16[4096,96]{0,1:T(8,128)(2,1)S(1)}, u32[]{:S(2)}) copy-start(bf16[4096,96]{0,1:T(8,128)(2,1)S(1)} %copy.25) | copy-start | bytes 2359300
  136.9 0.7 copy-start.26
  140.9 2.9 copy-start.3
  143.8 2.0 copy-start.38
  145.5 28.2 %copy-start.5 = (bf16[4096,96]{0,1:T(8,128)(2,1)}, bf16[4096,96]{0,1:T(8,128)(2,1)S(1)}, u32[]{:S(2)}) copy-start(bf16[4096,96]{0,1:T(8,128)(2,1)S(1)} %get-tuple-element.102) | copy-start | bytes 2359300
  145.8 1.2 copy-start.19
  145.9 1.2 copy-start.41
  147.1 4.9 copy-start.7
  152.0 1.8 copy-start.42
  153.8 1.2 copy-start.17
  153.8 1.2 copy-start.31
  153.8 1.2 copy-start.33
  157.1 11.3 %copy-start.20 = (bf16[4096,96]{1,0:T(8,128)(2,1)S(1)}, bf16[4096,96]{1,0:T(8,128)(2,1)}, u32[]{:S(2)}) copy-start(bf16[4096,96]{1,0:T(8,128)(2,1)} %copy-done.18) | copy-start | bytes 2359300
  157.1 10.5 %collective-permute-start.4 = (bf16[4,8,6144]{2,1,0:T(8,128)(2,1)S(1)}, bf16[4,8,6144]{2,1,0:T(8,128)(2,1)S(1)}, u32[]{:S(2)}, u32[]{:S(2)}) collective-permute-start(bf16[4,8,6144]{2,1,0:T(8,128)(2,1)S(1)} %slice.123), channel_id=1, source_target_pairs={{0,248},{8,0},{16,8},{24,16},{32,24},{40,32},{48,40},{56,48},{64,5... | collective-permute-start | bytes 1179656 | tf_op jit(solution)/shard_map/ppermute | solution.py:19
  168.0 5.8 copy-start.43
  168.0 15.8 %collective-permute-start.5 = (bf16[8,4,6144]{2,1,0:T(4,128)(2,1)S(1)}, bf16[8,4,6144]{2,1,0:T(4,128)(2,1)S(1)}, u32[]{:S(2)}, u32[]{:S(2)}) collective-permute-start(bf16[8,4,6144]{2,1,0:T(4,128)(2,1)S(1)} %get-tuple-element.108), channel_id=1, source_target_pairs={{0,7},{1,0},{2,1},{3,2},{4,3},{5,4},{6,5},{7,6},{8,15},{9,8},{10,9... | collective-permute-start | bytes 1179656 | tf_op jit(solution)/shard_map/ppermute | solution.py:19
  185.3 1.1 copy-start.11
  187.2 1.2 copy-start.21
  195.5 2.8 copy-start.22
  198.3 1.2 copy-start.21
  206.4 2.9 copy-start.22
  209.2 1.2 copy-start.21
  217.4 2.9 copy-start.22
  220.2 1.2 copy-start.21
  228.3 2.9 copy-start.22
  231.2 1.2 copy-start.21
  239.4 2.9 copy-start.22
  242.3 1.2 copy-start.21
  250.4 2.8 copy-start.22
  253.2 1.2 copy-start.21
  261.4 2.8 copy-start.22
  264.2 1.2 copy-start.21
  272.4 2.8 copy-start.22
  279.7 2.6 copy-start.14
  282.3 1.4 copy-start.28
  289.6 2.6 copy-start.10
  289.6 2.6 copy-start.12
  291.9 264.8 %collective-permute-start.6 = (bf16[8,4,6144]{2,1,0:T(4,128)(2,1)S(1)}, bf16[8,4,6144]{2,1,0:T(4,128)(2,1)}, u32[]{:S(2)}, u32[]{:S(2)}) collective-permute-start(bf16[8,4,6144]{2,1,0:T(4,128)(2,1)S(1)} %fusion.75), channel_id=1, source_target_pairs={{0,1},{1,2},{2,3},{3,4},{4,5},{5,6},{6,7},{7,0},{8,9},{9,10},{10,1... | collective-permute-start | bytes 1179656 | tf_op jit(solution)/shard_map/ppermute | solution.py:19
  556.7 2.3 copy-start.36
  556.7 2.9 copy-start.35
  558.2 5.5 collective-permute-start.7
  566.0 2.9 copy-start.4
  566.0 2.9 copy-start.25
  566.0 2.9 copy-start.30
  568.9 2.2 copy-start.40
  568.9 83.5 %copy-start.6 = (bf16[4096,96]{0,1:T(8,128)(2,1)S(1)}, bf16[4096,96]{0,1:T(8,128)(2,1)}, u32[]{:S(2)}) copy-start(bf16[4096,96]{0,1:T(8,128)(2,1)} %copy-done.5) | copy-start | bytes 2359300
  568.9 83.5 %copy-start.16 = (bf16[4096,96]{0,1:T(8,128)(2,1)S(1)}, bf16[4096,96]{0,1:T(8,128)(2,1)}, u32[]{:S(2)}) copy-start(bf16[4096,96]{0,1:T(8,128)(2,1)} %copy-done.15) | copy-start | bytes 2359300
  568.9 83.5 %copy-start.32 = (f32[4096]{0:T(1024)S(1)}, f32[4096]{0:T(1024)}, u32[]{:S(2)}) copy-start(f32[4096]{0:T(1024)} %copy-done.31) | copy-start | bytes 49156
  568.9 83.5 %copy-start.34 = (f32[4096]{0:T(1024)S(1)}, f32[4096]{0:T(1024)}, u32[]{:S(2)}) copy-start(f32[4096]{0:T(1024)} %copy-done.33) | copy-start | bytes 49156
  652.5 7.8 %copy-start.1 = (bf16[96,384]{1,0:T(8,128)(2,1)S(1)}, bf16[96,384]{1,0:T(8,128)(2,1)}, u32[]{:S(2)}) copy-start(bf16[96,384]{1,0:T(8,128)(2,1)} %param.18) | copy-start | bytes 221188
  (10 other events, 7.0 us)
Sparse Core Ops, SparseCore 0:
  292.4 262.7 all-reduce.3
where the time goes:
time: 674 us; the launch traced here: 667 us
  waiting for transfers between devices  305 us (45%)
  matrix products  105 us (16%)
  local copies, waits for them, and re-layouts  89.9 us (13%)
  blocking collectives  79.7 us (12%)
  starting transfers between devices  38.2 us (6%)
  other arithmetic  33.9 us (5%)
  between operations  15 us (2%)
    psum x1, waiting for transfers between devices, local(): lax.psum((sum_attn, sum_proj, sum_expand, sum_reduce, sum_one, sum_two),...  262 us
    psum x1, blocking collectives, local(): lax.psum((sum_attn, sum_proj, sum_expand, sum_reduce, sum_one, sum_two),...  79.7 us
    ppermute x8, waiting for transfers between devices, shifted(): return lax.ppermute(value, axis, pairs)  42.4 us
    ppermute x8, starting transfers between devices, shifted(): return lax.ppermute(value, axis, pairs)  38.1 us
    dot_general x8, matrix products, attend_back(): jnp.einsum('hqk,hkd->hqd', grad_scores, parts[1], preferred_element_type=...  25.3 us
    dot_general x8, matrix products, attend_back(): jnp.einsum('hqk,hqd->hkd', grad_scores, parts[0], preferred_element_type=...  24.5 us
    dynamic_slice x16, local copies, waits for them, and re-layouts, local(): mixed_win, probs_win = lax.map(attend, packed_win)  17.2 us
    dot_general x8, matrix products, attend_back(): jnp.einsum('hqk,hqd->hkd', probs, grad_heads, preferred_element_type=jnp....  16.3 us
  transfers between devices with their start and end apart: 9, of which 8 were waited for; matrix products, arithmetic and copies ran while one was open for 2% of the time, Pallas kernels for 0%

commit v1 on v0

v1 whole, which is shorter than its diff:
```python
import math

import jax
import jax.numpy as jnp
from jax import lax
from jax.experimental import pallas as pl
from jax.experimental.pallas import tpu as pltpu
from jax.sharding import PartitionSpec as P

D = 96
HEADS = 3
HD = 32
WIN = 8
HID = 384
TOK = 512
CH = 384
EPS = 1e-05
F32 = jnp.float32
BF = jnp.bfloat16
SCALE = HD**-0.5
LOG2E = 1.4426950408889634
GC = math.sqrt(2.0 / math.pi)


def nn(a, b):
    return lax.dot_general(a, b, (((1,), (0,)), ((), ())), preferred_element_type=F32)


def nt(a, b):
    return lax.dot_general(a, b, (((1,), (1,)), ((), ())), preferred_element_type=F32)


def wide(col):
    return jnp.concatenate([col] * (TOK // 128), axis=1)


def fold(v):
    return v[:, 0:128] + v[:, 128:256] + v[:, 256:384] + v[:, 384:512]


def mean0(v):
    return jnp.sum(v, axis=0, keepdims=True) * (1.0 / D)


def norm_cols(v, gain):
    c = v - mean0(v)
    r = lax.rsqrt(mean0(c * c) + EPS)
    n = c * r
    return n * gain, n, r


def norm_back(dh, n, r, gain):
    e = dh * gain
    return r * (e - mean0(e) - n * mean0(e * n))


def load_window(ref, lo, hi):
    a = ref[:, :, pl.ds(lo, CH)].astype(F32).reshape(64, CH)
    b = ref[:, :, pl.ds(hi, CH)].astype(F32).reshape(64, CH)
    t = jnp.concatenate([a, b], axis=0).T
    return jnp.concatenate([t[0:96], t[96:192], t[192:288], t[288:384]], axis=1)


def store_window(ref, lo, hi, v):
    t = jnp.concatenate([v[:, 128 * i : 128 * (i + 1)] for i in range(4)], axis=0).T
    ref[:, :, pl.ds(lo, CH)] = t[0:64].reshape(8, 8, CH).astype(BF)
    ref[:, :, pl.ds(hi, CH)] = t[64:128].reshape(8, 8, CH).astype(BF)


def only_head(v, h):
    zero = jnp.zeros((HD, v.shape[1]), v.dtype)
    rows = [v[HD * h : HD * (h + 1)] if i == h else zero for i in range(HEADS)]
    return jnp.concatenate(rows, axis=0)


def offsets(w):
    lo = pl.multiple_of((2 * w + 1) * CH, 128)
    hi = pl.multiple_of(lax.rem(2 * w + 2, 16) * CH, 128)
    return lo, hi


def kernel(
    x_ref, g_ref, gain1, gain2, wa, wat, wp, wpt, we, wet, wr,
    out_ref, s_red, s_exp, s_proj, s_two, s_attn, s_one,
    probs, packed, vnat, h1s, n1s, r1s, dy1s, dmixs, deltas,
):
    s_red[...] = jnp.zeros_like(s_red)
    s_exp[...] = jnp.zeros_like(s_exp)
    s_proj[...] = jnp.zeros_like(s_proj)
    s_two[...] = jnp.zeros_like(s_two)
    s_attn[...] = jnp.zeros_like(s_attn)
    s_one[...] = jnp.zeros_like(s_one)

    def front(w, carry):
        lo, hi = offsets(w)
        x = load_window(x_ref, lo, hi)
        h1f, n1, r1 = norm_cols(x, wide(gain1[...]))
        h1 = h1f.astype(BF)
        h1s[w] = h1
        n1s[w] = n1
        r1s[w] = jnp.broadcast_to(r1, (8, TOK))
        pk = nn(wat[...], h1).astype(BF)
        packed[w] = pk
        qt, vt = pk[0:96], pk[192:288]
        kn = pk[96:192].T
        vnat[w] = vt.T
        mixed = []
        for h in range(HEADS):
            qm = only_head(qt, h)
            parts = []
            for c in range(2):
                cols = slice(256 * c, 256 * (c + 1))
                s = nn(kn, qm[:, cols])
                m = jnp.max(s, axis=0, keepdims=True)
                e = jnp.exp2((s - m) * (SCALE * LOG2E))
                inv = 1.0 / jnp.sum(e, axis=0, keepdims=True)
                p = (e * inv).astype(BF)
                probs[w * HEADS + h, :, cols] = p
                parts.append(nn(vt[HD * h : HD * (h + 1)], p))
            mixed.append(jnp.concatenate(parts, axis=1))
        mixed_f = jnp.concatenate(mixed, axis=0)
        mixed = mixed_f.astype(BF)
        branch = nn(wpt[...], mixed).astype(BF)
        y1 = (x + branch.astype(F32)).astype(BF).astype(F32)
        gain_b = wide(gain2[...])
        h2f, n2, r2 = norm_cols(y1, gain_b)
        h2 = h2f.astype(BF)
        u = nn(wet[...], h2)
        u2 = u * u
        t = jnp.tanh(u * (GC + (GC * 0.044715) * u2))
        half = 0.5 + 0.5 * t
        act = (u * half).astype(BF)
        slope = half + (0.5 * u) * (1.0 - t * t) * (GC + (3 * 0.044715 * GC) * u2)
        gf = load_window(g_ref, lo, hi)
        gb = gf.astype(BF)
        s_red[...] += nt(gb, act)
        du = (nn(wr[...], gb) * slope).astype(BF)
        s_exp[...] += nt(h2, du)
        dh2 = nn(we[...], du)
        s_two[...] += fold(dh2 * n2)
        dy1 = gf + norm_back(dh2, n2, r2, gain_b)
        dy1s[w] = dy1
        da = dy1.astype(BF)
        s_proj[...] += nt(mixed, da)
        dmix = nn(wp[...], da).astype(BF)
        dmixs[w] = dmix
        prod = dmix.astype(F32) * mixed_f
        rows = [jnp.sum(prod[HD * h : HD * (h + 1)], axis=0, keepdims=True) for h in range(HEADS)]
        deltas[w] = jnp.concatenate(rows + [jnp.zeros((8 - HEADS, TOK), F32)], axis=0)
        return carry

    lax.fori_loop(0, 8, front, 0)

    def back(w, carry):
        lo, hi = offsets(w)
        pk = packed[w]
        qt, kt = pk[0:96], pk[96:192]
        vn = vnat[w]
        dmix = dmixs[w]
        delta = deltas[w]
        dqs, dks, dvs = [], [], []
        for h in range(HEADS):
            rows = slice(HD * h, HD * (h + 1))
            dm = only_head(dmix, h)
            dq, dk, dv = [], 0.0, 0.0
            for c in range(2):
                cols = slice(256 * c, 256 * (c + 1))
                p = probs[w * HEADS + h, :, cols]
                dp = nn(vn, dm[:, cols])
                ds = (p.astype(F32) * (dp - delta[h : h + 1, cols]) * SCALE).astype(BF)
                dq.append(nn(kt[rows], ds))
                dk = dk + nt(qt[rows, cols], ds)
                dv = dv + nt(dmix[rows, cols], p)
            dqs.append(jnp.concatenate(dq, axis=1))
            dks.append(dk)
            dvs.append(dv)
        dpk = jnp.concatenate(dqs + dks + dvs, axis=0).astype(BF)
        s_attn[...] += nt(h1s[w], dpk)
        dh1 = nn(wa[...], dpk).astype(BF).astype(F32)
        n1 = n1s[w]
        s_one[...] += fold(dh1 * n1)
        r1 = r1s[w][0:1]
        store_window(out_ref, lo, hi, dy1s[w] + norm_back(dh1, n1, r1, wide(gain1[...])))
        return carry

    lax.fori_loop(0, 8, back, 0)


def compute(x, g, gain_one, gain_two, attn_weight, proj_weight, expand_weight, reduce_weight):
    vm = pl.BlockSpec(memory_space=pltpu.VMEM)
    shape = jax.ShapeDtypeStruct
    col = lambda v: jnp.broadcast_to(v[:, None], (D, 128))
    return pl.pallas_call(
        kernel,
        in_specs=[vm] * 11,
        out_specs=[vm] * 7,
        out_shape=[
            shape((8, 8, 6144), BF),
            shape((D, HID), F32),
            shape((D, HID), F32),
            shape((D, D), F32),
            shape((D, 128), F32),
            shape((D, 3 * D), F32),
            shape((D, 128), F32),
        ],
        scratch_shapes=[
            pltpu.VMEM((24, TOK, TOK), BF),
            pltpu.VMEM((8, 3 * D, TOK), BF),
            pltpu.VMEM((8, TOK, D), BF),
            pltpu.VMEM((8, D, TOK), BF),
            pltpu.VMEM((8, D, TOK), F32),
            pltpu.VMEM((8, 8, TOK), F32),
            pltpu.VMEM((8, D, TOK), F32),
            pltpu.VMEM((8, D, TOK), BF),
            pltpu.VMEM((8, 8, TOK), F32),
        ],
        compiler_params=pltpu.CompilerParams(vmem_limit_bytes=56 * 1024 * 1024),
        name="block_backward",
    )(
        x, g, col(gain_one), col(gain_two),
        attn_weight, attn_weight.T, proj_weight, proj_weight.T,
        expand_weight, expand_weight.T, reduce_weight,
    )


def shifted(value, axis, steps):
    count = lax.axis_size(axis)
    return lax.ppermute(value, axis, [(s, (s + steps) % count) for s in range(count)])


def ahead(v):
    v = jnp.concatenate([v[4:], shifted(v[:4], "gx", -1)], axis=0)
    return jnp.concatenate([v[:, 4:], shifted(v[:, :4], "gy", -1)], axis=1)


def behind(v):
    v = jnp.concatenate([shifted(v[:, 4:], "gy", 1), v[:, :4]], axis=1)
    return jnp.concatenate([shifted(v[4:], "gx", 1), v[:4]], axis=0)


def local(tokens, upstream, gain_one, gain_two, attn_weight, proj_weight, expand_weight, reduce_weight):
    count = tokens.shape[0] * tokens.shape[1] * (tokens.shape[2] // D)
    factor = 1.0 / math.sqrt(count * lax.axis_size("gx") * lax.axis_size("gy"))
    outs = compute(
        ahead(tokens), ahead(upstream), gain_one, gain_two,
        attn_weight, proj_weight, expand_weight, reduce_weight,
    )
    grad = behind(outs[0])
    red, exp, proj, two, attn, one = lax.psum(
        (outs[1], outs[2], outs[3], jnp.sum(outs[4], axis=1), outs[5], jnp.sum(outs[6], axis=1)),
        ("gx", "gy"),
    )
    return (grad, one * factor, two * factor, attn * factor, proj * factor, exp * factor, red.T * factor)


def solution(mesh):
    return jax.shard_map(
        local,
        mesh=mesh,
        in_specs=(P("gx", "gy", None), P("gx", "gy", None), P(), P(), P(), P(), P(), P()),
        out_specs=(P("gx", "gy", None), P(), P(), P(), P(), P(), P()),
        check_vma=False,
    )
```

time: 674 us -> 392 us (0.58)
  waiting for transfers between devices: 305 us -> 185 us
  matrix products: 105 us -> 0 us
  local copies, waits for them, and re-layouts: 89.9 us -> 7.47 us
  Pallas kernels: 0 us -> 58.3 us
  other arithmetic: 33.9 us -> 9.05 us
  starting transfers between devices: 38.2 us -> 18.8 us
  blocking collectives: 79.7 us -> 98.4 us
    dot_general x51 -> x0, matrix products: 95.4 us -> none  [the longest x8 25.3 us: attend_back(): jnp.einsum('hqk,hkd->hqd', grad_scores, parts[1], preferred_element_type=...]
    psum x1, waiting for transfers between devices: 262 us -> 171 us  [local(): lax.psum((outs[1], outs[2], outs[3], jnp.sum(outs[4], axis=1), outs[5], j...]
    pallas_call x0 -> x1, Pallas kernels: none -> 58.3 us  [compute(): pl.pallas_call(kernel, in_specs=[vm] * 11, out_specs=[vm] * 7, out_shape=...]
    ppermute x8 -> x6, waiting for transfers between devices: 42.4 us -> 13.9 us  [shifted(): lax.ppermute(value, axis, [(s, (s + steps) % count) for s in range(count)])]
    convert_element_type x11 -> x0, local copies, waits for them, and re-layouts: 22.7 us -> none  [the longest x2 5.07 us: local(): grad_h1.astype(jnp.float32)]
    ppermute x8 -> x6, starting transfers between devices: 38.1 us -> 18.8 us  [shifted(): lax.ppermute(value, axis, [(s, (s + steps) % count) for s in range(count)])]
    psum x1, blocking collectives: 79.7 us -> 98.4 us  [local(): lax.psum((outs[1], outs[2], outs[3], jnp.sum(outs[4], axis=1), outs[5], j...]
    dynamic_slice x24 -> x0, local copies, waits for them, and re-layouts: 17.4 us -> none  [the longest x16 17.2 us: local(): mixed_win, probs_win = lax.map(attend, packed_win)]
  transfers between devices with their start and end apart: 9 -> 7, of which waited for: 8 -> 3; matrix products, arithmetic and copies ran while one was open for 2% -> 2% of each run, Pallas kernels for 0% -> 0%
where the time goes in v1:
time: 392 us; the launch traced here: 391 us
  waiting for transfers between devices  185 us (47%)
  blocking collectives  98.4 us (25%)
  Pallas kernels  58.3 us (15%)
  starting transfers between devices  18.8 us (5%)
  between operations  14.2 us (4%)
  other arithmetic  9.05 us (2%)
  local copies, waits for them, and re-layouts  7.47 us (2%)
    psum x1, waiting for transfers between devices, local(): lax.psum((outs[1], outs[2], outs[3], jnp.sum(outs[4], axis=1), outs[5], j...  171 us
    psum x1, blocking collectives, local(): lax.psum((outs[1], outs[2], outs[3], jnp.sum(outs[4], axis=1), outs[5], j...  98.4 us
    pallas_call x1, Pallas kernels, compute(): pl.pallas_call(kernel, in_specs=[vm] * 11, out_specs=[vm] * 7, out_shape=...  58.3 us
    ppermute x6, starting transfers between devices, shifted(): lax.ppermute(value, axis, [(s, (s + steps) % count) for s in range(count)])  18.8 us
    ppermute x6, waiting for transfers between devices, shifted(): lax.ppermute(value, axis, [(s, (s + steps) % count) for s in range(count)])  13.9 us
  transfers between devices with their start and end apart: 7, of which 3 were waited for; matrix products, arithmetic and copies ran while one was open for 2% of the time, Pallas kernels for 0%

profile of v1, /device:TPU:1, one launch (start us, length us, event | category | flops | bytes accessed | tf_op | source)
XLA Modules:
  0.0 391.2 jit_solution(7383174710309640471)
XLA Ops:
  7.2 0.0 copy-start
  7.2 0.0 all-reduce.4.cloned.1.call-start
  7.2 1.2 fusion.6
  8.5 0.0 copy-start.3
  8.5 0.0 copy-start.1
  8.5 0.0 copy-start.4
  8.5 0.0 copy-start.2
  8.5 3.3 collective-permute-start
  11.8 0.0 copy-done
  11.8 0.1 fusion.5
  11.8 4.9 %collective-permute-start.2 = (bf16[4,8,6144]{2,1,0:T(8,128)(2,1)S(1)}, bf16[4,8,6144]{2,1,0:T(8,128)(2,1)S(1)}, u32[]{:S(2)}, u32[]{:S(2)}) collective-permute-start(bf16[4,8,6144]{2,1,0:T(8,128)(2,1)S(1)} %get-tuple-element.32), channel_id=1, source_target_pairs={{0,248},{8,0},{16,8},{24,16},{32,24},{40,32},{48,40},{56,48},{64,5... | collective-permute-start | bytes 1179656 | tf_op jit(solution)/shard_map/ppermute | solution.py:228
  16.7 0.0 copy-done.3
  16.7 0.7 copy.16
  17.4 0.0 copy-done.1
  17.4 0.7 copy.15
  18.2 0.0 copy-done.4
  18.2 0.8 copy.18.wr
  18.9 0.0 copy-done.2
  18.9 0.7 copy.17
  19.7 0.0 collective-permute-done
  19.7 0.3 fusion.3
  19.9 6.5 %collective-permute-start.1 = (bf16[8,4,6144]{2,1,0:T(4,128)(2,1)S(1)}, bf16[8,4,6144]{2,1,0:T(4,128)(2,1)S(1)}, u32[]{:S(2)}, u32[]{:S(2)}) collective-permute-start(bf16[8,4,6144]{2,1,0:T(4,128)(2,1)S(1)} %get-tuple-element.34), channel_id=1, source_target_pairs={{0,7},{1,0},{2,1},{3,2},{4,3},{5,4},{6,5},{7,6},{8,15},{9,8},{10,9... | collective-permute-start | bytes 1179656 | tf_op jit(solution)/shard_map/ppermute | solution.py:228
  26.4 0.0 collective-permute-done.2
  26.4 0.3 fusion.2
  26.8 3.6 collective-permute-start.3
  30.4 3.7 collective-permute-done.1
  34.0 1.3 pad_maximum_fusion.1.x_ref
  35.3 10.2 %collective-permute-done.3 = bf16[8,4,6144]{2,1,0:T(4,128)(2,1)S(1)} collective-permute-done((bf16[8,4,6144]{2,1,0:T(4,128)(2,1)S(1)}, bf16[8,4,6144]{2,1,0:T(4,128)(2,1)S(1)}, u32[]{:S(2)}, u32[]{:S(2)}) %collective-permute-start.3) | collective-permute-done | bytes 393248 | tf_op jit(solution)/shard_map/ppermute | solution.py:228
  45.5 0.0 copy-start.8
  45.5 0.0 copy-start.9
  45.5 1.3 pad_maximum_fusion.2.g_ref
  46.8 0.0 copy-done.8
  46.8 0.7 broadcast_in_dim.4.gain1
  47.5 0.0 copy-done.9
  47.5 0.7 broadcast_in_dim.5.gain2
  48.2 58.3 %block_backward.1 = (bf16[8,8,6144]{2,1,0:T(8,128)(2,1)}, f32[96,384]{1,0:T(8,128)}, f32[96,384]{1,0:T(8,128)}, f32[96,96]{1,0:T(8,128)}, f32[96,128]{1,0:T(8,12...) custom-call(bf16[8,8,6144]{2,1,0:T(8,128)(2,1)} %pad_maximum_fusion.1.x_ref, bf16[8,8,6144]{2,1,0:T(8,128)(2,1)} %pad_maximum_fusion.2.g_ref, ...), custom_call_target="tpu_custom_call" | custom-call | tf_op jit(solution)/shard_map/block_backward/pallas_call | solution.py:193
  106.4 0.0 copy-start.7
  106.4 0.0 copy-start.6
  106.5 0.0 copy-start.5
  106.5 1.8 fusion.4
  108.3 0.0 copy-done.7
  108.3 0.1 reduce_sum.18
  108.4 0.0 copy-done.6
  108.4 0.1 reduce_sum.19
  108.5 0.1 collective-permute-start.4
  108.6 0.0 all-reduce.4.cloned.1.call-update
  108.6 0.0 copy-done.5
  108.6 98.4 %all-reduce = (f32[96]{0:T(128)S(1)}, f32[96]{0:T(128)S(1)}, f32[96,96]{1,0:T(8,128)S(1)}) all-reduce(f32[96]{0:T(128)S(1)} %reduce_sum.18, f32[96]{0:T(128)S(1)} %reduce_sum.19, f32[96,96]{1,0:T(8,128)S(1)} %copy-done.5), channel_id=1, replica_groups=mesh['gx'=32,'gy'=8] {'gx','gy'}, use_global_device_ids=true, to_apply=%region_1.0 | all-reduce | flops 9408 | bytes 75264 | tf_op jit(solution)/shard_map/psum | solution.py:249
  207.0 0.5 broadcast_multiply_fusion.3
  207.5 0.6 broadcast_multiply_fusion.2
  208.2 0.0 collective-permute-done.4
  208.2 0.2 fusion.1
  208.4 0.5 collective-permute-start.5
  208.8 171.2 %all-reduce.4.cloned.1.call-done = (f32[96,288]{1,0:T(8,128)}, f32[96,384]{1,0:T(8,128)}, f32[96,384]{1,0:T(8,128)}) async-done(((f32[96,288]{1,0:T(8,128)}, f32[96,384]{1,0:T(8,128)}, f32[96,384]{1,0:T(8,128)}), (f32[96,288]{1,0:T(8,128)}, f32[96,384]{1,0:T(8,128)}, f32[96,384]{1,0:T(8,128)})) %all-reduce.4.cloned.1.call-update) | async-done | bytes 405520 | tf_op jit(solution)/shard_map/psum | solution.py:249
  380.0 1.6 broadcast_multiply_fusion.1
  381.6 1.7 multiply_bitcast_fusion
  383.3 0.0 collective-permute-done.5
  383.3 1.1 fusion
Async XLA Ops:
  7.2 4.6 %copy-start = (bf16[8,8,6144]{2,1,0:T(8,128)(2,1)S(1)}, bf16[8,8,6144]{2,1,0:T(8,128)(2,1)}, u32[]{:S(2)}) copy-start(bf16[8,8,6144]{2,1,0:T(8,128)(2,1)} %param.9) | copy-start | bytes 2359300
  7.2 372.8 %all-reduce.4.cloned.1.call-start = ((), (), s32[]{:S(2)}) async-start(), calls=%async_computation | async-start | bytes 884736 | tf_op jit(solution)/shard_map/psum | solution.py:249
  8.5 8.3 %copy-start.3 = (bf16[96,96]{1,0:T(8,128)(2,1)S(1)}, bf16[96,96]{1,0:T(8,128)(2,1)}, u32[]{:S(2)}) copy-start(bf16[96,96]{1,0:T(8,128)(2,1)} %wp.1) | copy-start | bytes 55300
  8.5 9.0 %copy-start.1 = (bf16[96,288]{1,0:T(8,128)(2,1)S(1)}, bf16[96,288]{1,0:T(8,128)(2,1)}, u32[]{:S(2)}) copy-start(bf16[96,288]{1,0:T(8,128)(2,1)} %wa.1) | copy-start | bytes 165892
  8.5 9.7 %copy-start.4 = (bf16[384,96]{0,1:T(8,128)(2,1)S(1)}, bf16[384,96]{0,1:T(8,128)(2,1)}, u32[]{:S(2)}) copy-start(bf16[384,96]{0,1:T(8,128)(2,1)} %param.15) | copy-start | bytes 221188
  8.5 10.4 %copy-start.2 = (bf16[96,384]{1,0:T(8,128)(2,1)S(1)}, bf16[96,384]{1,0:T(8,128)(2,1)}, u32[]{:S(2)}) copy-start(bf16[96,384]{1,0:T(8,128)(2,1)} %we.1) | copy-start | bytes 221188
  8.5 11.2 %collective-permute-start = (bf16[4,8,6144]{2,1,0:T(8,128)(2,1)S(1)}, bf16[4,8,6144]{2,1,0:T(8,128)(2,1)S(1)}, u32[]{:S(2)}, u32[]{:S(2)}) collective-permute-start(bf16[4,8,6144]{2,1,0:T(8,128)(2,1)S(1)} %get-tuple-element.36), channel_id=1, source_target_pairs={{0,248},{8,0},{16,8},{24,16},{32,24},{40,32},{48,40},{56,48},{64,5... | collective-permute-start | bytes 1179656 | tf_op jit(solution)/shard_map/ppermute | solution.py:228
  11.8 14.6 %collective-permute-start.2 = (bf16[4,8,6144]{2,1,0:T(8,128)(2,1)S(1)}, bf16[4,8,6144]{2,1,0:T(8,128)(2,1)S(1)}, u32[]{:S(2)}, u32[]{:S(2)}) collective-permute-start(bf16[4,8,6144]{2,1,0:T(8,128)(2,1)S(1)} %get-tuple-element.32), channel_id=1, source_target_pairs={{0,248},{8,0},{16,8},{24,16},{32,24},{40,32},{48,40},{56,48},{64,5... | collective-permute-start | bytes 1179656 | tf_op jit(solution)/shard_map/ppermute | solution.py:228
  19.9 14.1 %collective-permute-start.1 = (bf16[8,4,6144]{2,1,0:T(4,128)(2,1)S(1)}, bf16[8,4,6144]{2,1,0:T(4,128)(2,1)S(1)}, u32[]{:S(2)}, u32[]{:S(2)}) collective-permute-start(bf16[8,4,6144]{2,1,0:T(4,128)(2,1)S(1)} %get-tuple-element.34), channel_id=1, source_target_pairs={{0,7},{1,0},{2,1},{3,2},{4,3},{5,4},{6,5},{7,6},{8,15},{9,8},{10,9... | collective-permute-start | bytes 1179656 | tf_op jit(solution)/shard_map/ppermute | solution.py:228
  26.8 18.7 %collective-permute-start.3 = (bf16[8,4,6144]{2,1,0:T(4,128)(2,1)S(1)}, bf16[8,4,6144]{2,1,0:T(4,128)(2,1)S(1)}, u32[]{:S(2)}, u32[]{:S(2)}) collective-permute-start(bf16[8,4,6144]{2,1,0:T(4,128)(2,1)S(1)} %get-tuple-element.30), channel_id=1, source_target_pairs={{0,7},{1,0},{2,1},{3,2},{4,3},{5,4},{6,5},{7,6},{8,15},{9,8},{10,9... | collective-permute-start | bytes 1179656 | tf_op jit(solution)/shard_map/ppermute | solution.py:228
  45.5 1.3 copy-start.8
  45.5 2.0 copy-start.9
  106.4 1.8 copy-start.7
  106.4 2.0 copy-start.6
  106.5 2.2 copy-start.5
  108.5 99.6 %collective-permute-start.4 = (bf16[8,4,6144]{2,1,0:T(4,128)(2,1)S(1)}, bf16[8,4,6144]{2,1,0:T(4,128)(2,1)S(1)}, u32[]{:S(2)}, u32[]{:S(2)}) collective-permute-start(bf16[8,4,6144]{2,1,0:T(4,128)(2,1)S(1)} %get-tuple-element.27), channel_id=1, source_target_pairs={{0,1},{1,2},{2,3},{3,4},{4,5},{5,6},{6,7},{7,0},{8,9},{9,10},{10,1... | collective-permute-start | bytes 1179656 | tf_op jit(solution)/shard_map/ppermute | solution.py:228
  208.4 174.9 %collective-permute-start.5 = (bf16[4,8,6144]{2,1,0:T(8,128)(2,1)S(1)}, bf16[4,8,6144]{2,1,0:T(8,128)(2,1)S(1)}, u32[]{:S(2)}, u32[]{:S(2)}) collective-permute-start(bf16[4,8,6144]{2,1,0:T(8,128)(2,1)S(1)} %fusion.1), channel_id=1, source_target_pairs={{0,8},{8,16},{16,24},{24,32},{32,40},{40,48},{48,56},{56,64},{64,7... | collective-permute-start | bytes 1179656 | tf_op jit(solution)/shard_map/ppermute | solution.py:228
Sparse Core Ops, SparseCore 0:
  108.8 271.2 all-reduce.3

commit v2 on v1

--- a/solution.py
+++ b/solution.py
@@ -1,3 +1,4 @@
+import functools
 import math
 
 import jax
@@ -54,6 +55,10 @@
     return r * (e - mean0(e) - n * mean0(e * n))
 
 
+def flip(v):
+    return v.astype(F32).T.astype(v.dtype)
+
+
 def load_window(ref, lo, hi):
     a = ref[:, :, pl.ds(lo, CH)].astype(F32).reshape(64, CH)
     b = ref[:, :, pl.ds(hi, CH)].astype(F32).reshape(64, CH)
@@ -79,11 +84,172 @@
     return lo, hi
 
 
+MESH = pl.DeviceIdType.MESH
+NGX, NGY = 32, 8
+GROUP = 16
+SHIFTS = ((1, 1), (0, 1), (1, 0))
+CUTS = (0, 5 * CH, 11 * CH, 16 * CH)
+READY = (0, 2, 5)
+ROWS_A, ROWS_B = 48, 24
+
+
+def half(flag):
+    return pl.ds(4, 4) if flag else pl.ds(0, 4)
+
+
+def place():
+    a, b = lax.axis_index("gx"), lax.axis_index("gy")
+    first = (b // 4) * 8 + lax.rem(a, 8)
+    second = (a // 8) * 4 + lax.rem(b, 4)
+    return a, b, first, second
+
+
+def device(first, second):
+    return ((second // 4) * 8 + lax.rem(first, 8), (first // 8) * 4 + lax.rem(second, 4))
+
+
+def neighbour(dx, dy):
+    a, b = lax.axis_index("gx"), lax.axis_index("gy")
+    return (lax.rem(a + dx + NGX, NGX), lax.rem(b + dy + NGY, NGY))
+
+
+def remote(src, dst, send, recv, where):
+    return pltpu.make_async_remote_copy(
+        src_ref=src, dst_ref=dst, send_sem=send, recv_sem=recv, device_id=where, device_id_type=MESH
+    )
+
+
+def halo_in(src, dst, send, recv, part, k):
+    dx, dy = SHIFTS[k]
+    cols = pl.ds(CUTS[part], CUTS[part + 1] - CUTS[part])
+    return remote(
+        src.at[half(not dx), half(not dy), cols], dst.at[half(dx), half(dy), cols],
+        send.at[part, k], recv.at[part, k], neighbour(-dx, -dy),
+    )
+
+
+def own_in(src, dst, sem, part):
+    cols = pl.ds(CUTS[part], CUTS[part + 1] - CUTS[part])
+    return pltpu.make_async_copy(
+        src.at[half(1), half(1), cols], dst.at[half(0), half(0), cols], sem.at[part]
+    )
+
+
+def halo_out(src, dst, send, recv, k, cols):
+    dx, dy = SHIFTS[k]
+    return remote(
+        src.at[half(dx), half(dy), cols], dst.at[half(not dx), half(not dy), cols],
+        send.at[k], recv.at[k], neighbour(dx, dy),
+    )
+
+
+def own_out(src, dst, sem, cols):
+    return pltpu.make_async_copy(
+        src.at[half(0), half(0), cols], dst.at[half(1), half(1), cols], sem
+    )
+
+
+def send_out(src, dst, send, recv, sem, cols):
+    for k in range(3):
+        halo_out(src, dst, send, recv, k, cols).start()
+    own_out(src, dst, sem, cols).start()
+
+
+def spread(src_of, dst, slot, send, recv, along_first):
+    a, b, first, second = place()
+    mine = first if along_first else second
+
+    def step(r, carry):
+        to = lax.rem(mine + r, GROUP)
+        where = device(to, second) if along_first else device(first, to)
+        remote(src_of(to), dst.at[slot], send, recv, where).start()
+        return carry
+
+    lax.fori_loop(1, GROUP, step, 0)
+
+
+def settle(buf, send, recv):
+    most = buf.at[pl.ds(0, GROUP - 1)]
+    done = remote(most, most, send, recv, neighbour(1, 0))
+    done.wait_recv()
+    done.wait_send()
+
+
+def total(buf):
+    acc = buf[0]
+    for i in range(1, GROUP):
+        acc = acc + buf[i]
+    return acc
+
+
+def reduce_start(parts, got, sems):
+    a, b, first, second = place()
+    got[first] = parts[first]
+    spread(lambda to: parts.at[to], got, first, sems.at[0, 0], sems.at[1, 0], True)
+
+
+def reduce_middle(got, cross, sems, factor):
+    a, b, first, second = place()
+    settle(got, sems.at[0, 0], sems.at[1, 0])
+    cross[second] = total(got) * factor
+    spread(lambda to: cross.at[second], cross, second, sems.at[0, 1], sems.at[1, 1], False)
+
+
+def reduce_last(cross, final, sems):
+    a, b, first, second = place()
+    settle(cross, sems.at[0, 1], sems.at[1, 1])
+    final[first] = total(cross)
+    spread(lambda to: final.at[first], final, first, sems.at[0, 2], sems.at[1, 2], True)
+
+
+def reduce_end(final, sems):
+    settle(final, sems.at[0, 2], sems.at[1, 2])
+
+
 def kernel(
-    x_ref, g_ref, gain1, gain2, wa, wat, wp, wpt, we, wet, wr,
-    out_ref, s_red, s_exp, s_proj, s_two, s_attn, s_one,
-    probs, packed, vnat, h1s, n1s, r1s, dy1s, dmixs, deltas,
+    factor, tok_ref, up_ref, gain1_ref, gain2_ref, wa, wp, we, wrt,
+    out_ref, o_one, o_two, o_attn, o_proj, o_exp, o_red,
+    rx, rg, ob, wat, wpt, wet, wr, gain1, gain2,
+    s_red, s_exp, s_proj, s_two, s_attn, s_one,
+    probs, packed, vnat, h1s, n1s, r1s, mixes, dy1s, dmixs, deltas,
+    a_parts, a_got, a_cross, a_final, b_parts, b_got, b_cross, b_final,
+    x_send, x_recv, g_send, g_recv, x_own, g_own, y_send, y_recv, y_own, a_sems, b_sems,
 ):
+    a, b, first, second = place()
+    barrier = pltpu.get_barrier_semaphore()
+    for dx, dy in SHIFTS:
+        for sign in (-1, 1):
+            pl.semaphore_signal(
+                barrier, inc=1, device_id=neighbour(sign * dx, sign * dy), device_id_type=MESH
+            )
+
+    def greet(r, carry):
+        pl.semaphore_signal(
+            barrier, inc=1, device_id=device(lax.rem(first + r, GROUP), second), device_id_type=MESH
+        )
+        pl.semaphore_signal(
+            barrier, inc=1, device_id=device(first, lax.rem(second + r, GROUP)), device_id_type=MESH
+        )
+        return carry
+
+    lax.fori_loop(1, GROUP, greet, 0)
+    for part in range(3):
+        own_in(tok_ref, rx, x_own, part).start()
+        own_in(up_ref, rg, g_own, part).start()
+    pl.semaphore_wait(barrier, 2 * len(SHIFTS) + 2 * (GROUP - 1))
+    for part in range(3):
+        for k in range(3):
+            halo_in(tok_ref, rx, x_send, x_recv, part, k).start()
+    for part in range(3):
+        for k in range(3):
+            halo_in(up_ref, rg, g_send, g_recv, part, k).start()
+
+    wat[...] = flip(wa[...])
+    wpt[...] = flip(wp[...])
+    wet[...] = flip(we[...])
+    wr[...] = flip(wrt[...])
+    gain1[...] = jnp.broadcast_to(gain1_ref[...], (128, D)).T
+    gain2[...] = jnp.broadcast_to(gain2_ref[...], (128, D)).T
     s_red[...] = jnp.zeros_like(s_red)
     s_exp[...] = jnp.zeros_like(s_exp)
     s_proj[...] = jnp.zeros_like(s_proj)
@@ -91,9 +257,17 @@
     s_attn[...] = jnp.zeros_like(s_attn)
     s_one[...] = jnp.zeros_like(s_one)
 
-    def front(w, carry):
+    def attend(w, carry):
+        for part in range(3):
+
+            @pl.when(w == READY[part])
+            def _(part=part):
+                own_in(tok_ref, rx, x_own, part).wait()
+                for k in range(3):
+                    halo_in(tok_ref, rx, x_send, x_recv, part, k).wait_recv()
+
         lo, hi = offsets(w)
-        x = load_window(x_ref, lo, hi)
+        x = load_window(rx, lo, hi)
         h1f, n1, r1 = norm_cols(x, wide(gain1[...]))
         h1 = h1f.astype(BF)
         h1s[w] = h1
@@ -119,6 +293,23 @@
                 parts.append(nn(vt[HD * h : HD * (h + 1)], p))
             mixed.append(jnp.concatenate(parts, axis=1))
         mixed_f = jnp.concatenate(mixed, axis=0)
+        mixes[w] = mixed_f
+        return carry
+
+    lax.fori_loop(0, 8, attend, 0)
+
+    def mlp(w, carry):
+        for part in range(3):
+
+            @pl.when(w == READY[part])
+            def _(part=part):
+                own_in(up_ref, rg, g_own, part).wait()
+                for k in range(3):
+                    halo_in(up_ref, rg, g_send, g_recv, part, k).wait_recv()
+
+        lo, hi = offsets(w)
+        x = load_window(rx, lo, hi)
+        mixed_f = mixes[w]
         mixed = mixed_f.astype(BF)
         branch = nn(wpt[...], mixed).astype(BF)
         y1 = (x + branch.astype(F32)).astype(BF).astype(F32)
@@ -128,10 +319,10 @@
         u = nn(wet[...], h2)
         u2 = u * u
         t = jnp.tanh(u * (GC + (GC * 0.044715) * u2))
-        half = 0.5 + 0.5 * t
-        act = (u * half).astype(BF)
-        slope = half + (0.5 * u) * (1.0 - t * t) * (GC + (3 * 0.044715 * GC) * u2)
-        gf = load_window(g_ref, lo, hi)
+        cdf = 0.5 + 0.5 * t
+        act = (u * cdf).astype(BF)
+        slope = cdf + (0.5 * u) * (1.0 - t * t) * (GC + (3 * 0.044715 * GC) * u2)
+        gf = load_window(rg, lo, hi)
         gb = gf.astype(BF)
         s_red[...] += nt(gb, act)
         du = (nn(wr[...], gb) * slope).astype(BF)
@@ -149,9 +340,32 @@
         deltas[w] = jnp.concatenate(rows + [jnp.zeros((8 - HEADS, TOK), F32)], axis=0)
         return carry
 
-    lax.fori_loop(0, 8, front, 0)
+    lax.fori_loop(0, 8, mlp, 0)
+
+    two = jnp.broadcast_to(jnp.sum(s_two[...], axis=1, keepdims=True), (D, 32))
+    tail = jnp.concatenate([s_proj[...], two], axis=1)
+    tiles = [s_red[:, 0:128], s_red[:, 128:256], s_red[:, 256:384]]
+    tiles += [s_exp[:, 0:128], s_exp[:, 128:256], s_exp[:, 256:384], tail]
+    for j in range(8):
+        for i in range(2):
+            rows = slice(ROWS_A * i, ROWS_A * (i + 1))
+            a_parts[2 * j + i] = tiles[j][rows] if j < 7 else jnp.zeros((ROWS_A, 128), F32)
+    reduce_start(a_parts, a_got, a_sems)
 
     def back(w, carry):
+        @pl.when(w > 0)
+        def _():
+            cols = pl.ds(pl.multiple_of((2 * w - 1) * CH, 128), 2 * CH)
+            send_out(ob, out_ref, y_send, y_recv, y_own, cols)
+
+        @pl.when(w == 3)
+        def _():
+            reduce_middle(a_got, a_cross, a_sems, factor)
+
+        @pl.when(w == 6)
+        def _():
+            reduce_last(a_cross, a_final, a_sems)
+
         lo, hi = offsets(w)
         pk = packed[w]
         qt, kt = pk[0:96], pk[96:192]
@@ -180,30 +394,81 @@
         n1 = n1s[w]
         s_one[...] += fold(dh1 * n1)
         r1 = r1s[w][0:1]
-        store_window(out_ref, lo, hi, dy1s[w] + norm_back(dh1, n1, r1, wide(gain1[...])))
+        store_window(ob, lo, hi, dy1s[w] + norm_back(dh1, n1, r1, wide(gain1[...])))
         return carry
 
     lax.fori_loop(0, 8, back, 0)
 
-
-def compute(x, g, gain_one, gain_two, attn_weight, proj_weight, expand_weight, reduce_weight):
+    one = jnp.broadcast_to(jnp.sum(s_one[...], axis=1, keepdims=True), (D, 96))
+    last = jnp.concatenate([s_attn[:, 256:288], one], axis=1)
+    tiles = [s_attn[:, 0:128], s_attn[:, 128:256], last]
+    for j in range(4):
+        for i in range(4):
+            rows = slice(ROWS_B * i, ROWS_B * (i + 1))
+            b_parts[4 * j + i] = tiles[j][rows] if j < 3 else jnp.zeros((ROWS_B, 128), F32)
+    reduce_start(b_parts, b_got, b_sems)
+    for start in (15 * CH, 0):
+        send_out(ob, out_ref, y_send, y_recv, y_own, pl.ds(start, CH))
+    reduce_middle(b_got, b_cross, b_sems, factor)
+    reduce_end(a_final, a_sems)
+    fa = [jnp.concatenate([a_final[2 * j], a_final[2 * j + 1]], axis=0) for j in range(7)]
+    o_red[...] = jnp.concatenate(fa[0:3], axis=1)
+    o_exp[...] = jnp.concatenate(fa[3:6], axis=1)
+    o_proj[...] = fa[6][:, 0:96]
+    o_two[...] = fa[6].T[96:97]
+    reduce_last(b_cross, b_final, b_sems)
+    for part in range(3):
+        for k in range(3):
+            halo_in(tok_ref, rx, x_send, x_recv, part, k).wait_send()
+            halo_in(up_ref, rg, g_send, g_recv, part, k).wait_send()
+    everything = pl.ds(0, 16 * CH)
+    own_out(ob, out_ref, y_own, everything).wait()
+    for k in range(3):
+        done = halo_out(ob, out_ref, y_send, y_recv, k, everything)
+        done.wait_send()
+        done.wait_recv()
+    reduce_end(b_final, b_sems)
+    fb = [jnp.concatenate([b_final[4 * j + i] for i in range(4)], axis=0) for j in range(3)]
+    o_attn[...] = jnp.concatenate([fb[0], fb[1], fb[2][:, 0:32]], axis=1)
+    o_one[...] = fb[2].T[32:33]
+
+
+def local(tokens, upstream, gain_one, gain_two, attn_weight, proj_weight, expand_weight, reduce_weight):
+    count = tokens.shape[0] * tokens.shape[1] * (tokens.shape[2] // D)
+    factor = 1.0 / math.sqrt(count * lax.axis_size("gx") * lax.axis_size("gy"))
     vm = pl.BlockSpec(memory_space=pltpu.VMEM)
+    hbm = pl.BlockSpec(memory_space=pl.ANY)
     shape = jax.ShapeDtypeStruct
-    col = lambda v: jnp.broadcast_to(v[:, None], (D, 128))
-    return pl.pallas_call(
-        kernel,
-        in_specs=[vm] * 11,
-        out_specs=[vm] * 7,
+    dma = pltpu.SemaphoreType.DMA
+    outs = pl.pallas_call(
+        functools.partial(kernel, factor),
+        in_specs=[hbm, hbm] + [vm] * 6,
+        out_specs=[hbm] + [vm] * 6,
         out_shape=[
             shape((8, 8, 6144), BF),
+            shape((1, D), F32),
+            shape((1, D), F32),
+            shape((D, 3 * D), F32),
+            shape((D, D), F32),
             shape((D, HID), F32),
             shape((D, HID), F32),
-            shape((D, D), F32),
-            shape((D, 128), F32),
-            shape((D, 3 * D), F32),
-            shape((D, 128), F32),
         ],
         scratch_shapes=[
+            pltpu.VMEM((8, 8, 6144), BF),
+            pltpu.VMEM((8, 8, 6144), BF),
+            pltpu.VMEM((8, 8, 6144), BF),
+            pltpu.VMEM((3 * D, D), BF),
+            pltpu.VMEM((D, D), BF),
+            pltpu.VMEM((HID, D), BF),
+            pltpu.VMEM((HID, D), BF),
+            pltpu.VMEM((D, 128), F32),
+            pltpu.VMEM((D, 128), F32),
+            pltpu.VMEM((D, HID), F32),
+            pltpu.VMEM((D, HID), F32),
+            pltpu.VMEM((D, D), F32),
+            pltpu.VMEM((D, 128), F32),
+            pltpu.VMEM((D, 3 * D), F32),
+            pltpu.VMEM((D, 128), F32),
             pltpu.VMEM((24, TOK, TOK), BF),
             pltpu.VMEM((8, 3 * D, TOK), BF),
             pltpu.VMEM((8, TOK, D), BF),
@@ -211,46 +476,26 @@
             pltpu.VMEM((8, D, TOK), F32),
             pltpu.VMEM((8, 8, TOK), F32),
             pltpu.VMEM((8, D, TOK), F32),
+            pltpu.VMEM((8, D, TOK), F32),
             pltpu.VMEM((8, D, TOK), BF),
             pltpu.VMEM((8, 8, TOK), F32),
-        ],
-        compiler_params=pltpu.CompilerParams(vmem_limit_bytes=56 * 1024 * 1024),
+        ]
+        + [pltpu.VMEM((GROUP, ROWS_A, 128), F32)] * 4
+        + [pltpu.VMEM((GROUP, ROWS_B, 128), F32)] * 4
+        + [dma((3, 3))] * 4
+        + [dma((3,))] * 2
+        + [dma((3,))] * 2
+        + [dma, dma((2, 3)), dma((2, 3))],
+        compiler_params=pltpu.CompilerParams(
+            vmem_limit_bytes=56 * 1024 * 1024, collective_id=0, has_side_effects=True
+        ),
         name="block_backward",
     )(
-        x, g, col(gain_one), col(gain_two),
-        attn_weight, attn_weight.T, proj_weight, proj_weight.T,
-        expand_weight, expand_weight.T, reduce_weight,
-    )
-
-
-def shifted(value, axis, steps):
-    count = lax.axis_size(axis)
-    return lax.ppermute(value, axis, [(s, (s + steps) % count) for s in range(count)])
-
-
-def ahead(v):
-    v = jnp.concatenate([v[4:], shifted(v[:4], "gx", -1)], axis=0)
-    return jnp.concatenate([v[:, 4:], shifted(v[:, :4], "gy", -1)], axis=1)
-
-
-def behind(v):
-    v = jnp.concatenate([shifted(v[:, 4:], "gy", 1), v[:, :4]], axis=1)
-    return jnp.concatenate([shifted(v[4:], "gx", 1), v[:4]], axis=0)
-
-
-def local(tokens, upstream, gain_one, gain_two, attn_weight, proj_weight, expand_weight, reduce_weight):
-    count = tokens.shape[0] * tokens.shape[1] * (tokens.shape[2] // D)
-    factor = 1.0 / math.sqrt(count * lax.axis_size("gx") * lax.axis_size("gy"))
-    outs = compute(
-        ahead(tokens), ahead(upstream), gain_one, gain_two,
-        attn_weight, proj_weight, expand_weight, reduce_weight,
-    )
-    grad = behind(outs[0])
-    red, exp, proj, two, attn, one = lax.psum(
-        (outs[1], outs[2], outs[3], jnp.sum(outs[4], axis=1), outs[5], jnp.sum(outs[6], axis=1)),
-        ("gx", "gy"),
-    )
-    return (grad, one * factor, two * factor, attn * factor, proj * factor, exp * factor, red.T * factor)
+        tokens, upstream, gain_one.reshape(1, D), gain_two.reshape(1, D),
+        attn_weight, proj_weight, expand_weight, reduce_weight.T,
+    )
+    grad, one, two, attn, proj, exp, red = outs
+    return (grad, one.reshape(D), two.reshape(D), attn, proj, exp, red.T)
 
 
 def solution(mesh):

time: 392 us -> 125 us (0.32)
  waiting for transfers between devices: 185 us -> 0 us
  blocking collectives: 98.4 us -> 0 us
  Pallas kernels: 58.3 us -> 118 us
  starting transfers between devices: 18.8 us -> 0 us
  between operations: 14.2 us -> 0.67 us
  other arithmetic: 9.05 us -> 0 us
    psum x1 -> x0, waiting for transfers between devices: 171 us -> none  [local(): lax.psum((outs[1], outs[2], outs[3], jnp.sum(outs[4], axis=1), outs[5], j...]
    psum x1 -> x0, blocking collectives: 98.4 us -> none  [local(): lax.psum((outs[1], outs[2], outs[3], jnp.sum(outs[4], axis=1), outs[5], j...]
    pallas_call x1, Pallas kernels: 58.3 us -> 118 us  [local(): pl.pallas_call(functools.partial(kernel, factor), in_specs=[hbm, hbm] + [...]
    ppermute x6 -> x0, starting transfers between devices: 18.8 us -> none  [shifted(): lax.ppermute(value, axis, [(s, (s + steps) % count) for s in range(count)])]
    ppermute x6 -> x0, waiting for transfers between devices: 13.9 us -> none  [shifted(): lax.ppermute(value, axis, [(s, (s + steps) % count) for s in range(count)])]
    mul x4 -> x0, other arithmetic: 4.43 us -> none  [the longest x1 1.71 us: local(): red.T * factor]
    concatenate x6 -> x0, other arithmetic: 4.42 us -> none  [the longest x2 2.54 us: ahead(): return jnp.concatenate([v[:, 4:], shifted(v[:, :4], 'gy', -1)], axis=1)]
  transfers between devices with their start and end apart: 7 -> 0, of which waited for: 3 -> 0; matrix products, arithmetic and copies ran while one was open for 2% -> 0% of each run, Pallas kernels for 0% -> 0%
where the time goes in v2:
time: 125 us
  Pallas kernels  118 us (94%)
  local copies, waits for them, and re-layouts  6.23 us (5%)
    pallas_call x1, Pallas kernels, local(): pl.pallas_call(functools.partial(kernel, factor), in_specs=[hbm, hbm] + [...  118 us
    unnamed x19, local copies, waits for them, and re-layouts  6.23 us

profile of v2, /device:TPU:1, one launch (start us, length us, event | category | flops | bytes accessed | tf_op | source)
XLA Modules:
  0.0 125.0 jit_solution(16240340025344205098)
XLA Ops:
  0.6 118.1 %block_backward.1 = (bf16[8,8,6144]{2,1,0:T(8,128)(2,1)}, f32[1,96]{1,0:T(1,128)}, f32[1,96]{1,0:T(1,128)}, f32[96,288]{1,0:T(8,128)}, f32[96,96]{1,0:T(8,128)}, /*index=5*/f32[96,384]{1,0:T(8,128)}, f32[96,384]{1,0:T(8,128)}) custom-call(bf16[8,8,6144]{2,1,0:T(8,128)(2,1)} %tok_ref.1, bf16[8,8,6144]{2,1,0:T(8,128)(2,1)} %up_ref.1, f32[1,96]{1,0:T(1,128)} %bitcast.8, ...), custom_call_target="tpu_custom_call" | custom-call | tf_op jit(solution)/shard_map/block_backward/pallas_call | solution.py:443
  118.8 0.0 copy-start.5
  118.8 0.0 copy-start.2
  118.8 2.1 %copy.22 = bf16[8,8,6144]{2,1,0:T(8,128)(2,1)} copy(bf16[8,8,6144]{2,1,0:T(8,128)(2,1)} %get-tuple-element.28) | data formatting | bytes 1572864
  120.9 0.0 copy-done.5
  120.9 0.0 copy-start.4
  120.9 0.5 copy.23
  121.4 0.1 copy-done.4
  121.5 0.5 copy.24
  122.0 0.0 copy-done.2
  122.0 0.0 copy-start.3
  122.0 0.0 copy-start.1
  122.0 0.7 copy.25
  122.7 0.1 copy-done.3
  122.8 0.6 copy.26
  123.4 0.0 copy-done.1
  123.4 0.0 copy-start
  123.4 0.7 copy.27
  124.1 0.3 copy-done
  124.4 0.7 copy.28
Async XLA Ops:
  118.8 2.1 %copy-start.5 = (f32[1,96]{1,0:T(1,128)S(1)}, f32[1,96]{1,0:T(1,128)}, u32[]{:S(2)}) copy-start(f32[1,96]{1,0:T(1,128)} %get-tuple-element.15) | copy-start | bytes 1156
  118.8 3.2 %copy-start.2 = (f32[96,288]{1,0:T(8,128)S(1)}, f32[96,288]{1,0:T(8,128)}, u32[]{:S(2)}) copy-start(f32[96,288]{1,0:T(8,128)} %get-tuple-element.31) | copy-start | bytes 331780
  120.9 0.6 copy-start.4
  122.0 0.8 copy-start.3
  122.0 1.4 %copy-start.1 = (f32[96,384]{1,0:T(8,128)S(1)}, f32[96,384]{1,0:T(8,128)}, u32[]{:S(2)}) copy-start(f32[96,384]{1,0:T(8,128)} %get-tuple-element.33) | copy-start | bytes 442372
  123.4 1.0 copy-start

commit v3 on v2

--- a/solution.py
+++ b/solution.py
@@ -88,9 +88,13 @@
 NGX, NGY = 32, 8
 GROUP = 16
 SHIFTS = ((1, 1), (0, 1), (1, 0))
-CUTS = (0, 5 * CH, 11 * CH, 16 * CH)
-READY = (0, 2, 5)
-ROWS_A, ROWS_B = 48, 24
+RELAYS = ((0, 3), (0, 4), (1, 4), (1, -3))
+CUTS = (0, 3 * CH, 7 * CH, 13 * CH, 16 * CH)
+PARTS = 4
+READY = (0, 1, 3, 6)
+FORWARD = (0, 1, 2, 3)
+ROWS_A, ROWS_B = 48, 16
+RELAY_STEP, RELAY_NEXT, RELAY_AT = 3, 4, 3
 
 
 def half(flag):
@@ -128,6 +132,25 @@
     )
 
 
+def relay_in(src, dst, send, recv, part, k):
+    dx, dy = SHIFTS[k]
+    cols = pl.ds(CUTS[part], CUTS[part + 1] - CUTS[part])
+    a, b = neighbour(-dx, RELAY_STEP)
+    return remote(
+        src.at[half(not dx), half(not dy), cols], dst.at[half(dx), half(dy), cols],
+        send.at[part, k], recv.at[part, k], (a, b),
+    )
+
+
+def relay_on(src, dst, send, recv, part, k):
+    dx, dy = SHIFTS[k]
+    cols = pl.ds(CUTS[part], CUTS[part + 1] - CUTS[part])
+    box = (half(dx), half(dy), cols)
+    return remote(
+        src.at[box], dst.at[box], send.at[part, k], recv.at[part, k], neighbour(0, RELAY_NEXT)
+    )
+
+
 def own_in(src, dst, sem, part):
     cols = pl.ds(CUTS[part], CUTS[part + 1] - CUTS[part])
     return pltpu.make_async_copy(
@@ -206,14 +229,143 @@
     settle(final, sems.at[0, 2], sems.at[1, 2])
 
 
+def attn_forward(w, qt, kn, vt, probs, sbuf):
+    units = [(h, c) for h in range(HEADS) for c in range(2)]
+    top, mixed = {}, {}
+    sums = {}
+
+    def rows_of(j):
+        return slice(64 * j, 64 * (j + 1))
+
+    def score(t, j):
+        h, c = units[t]
+        s = nn(kn[rows_of(j)], heads[h][:, 256 * c : 256 * (c + 1)])
+        sbuf[t % 3, rows_of(j), :] = s
+        m = jnp.max(s.reshape(64 // 8, 8, 256), axis=0)
+        top[t] = m if j == 0 else jnp.maximum(top[t], m)
+
+    def power(t, j, m):
+        e = jnp.exp2((sbuf[t % 3, rows_of(j), :] - m) * (SCALE * LOG2E))
+        sbuf[t % 3, rows_of(j), :] = e
+        part = jnp.sum(e.reshape(64 // 8, 8, 256), axis=0)
+        sums[t] = part if j == 0 else sums[t] + part
+
+    def weigh(t, j, inv):
+        h, c = units[t]
+        p = (sbuf[t % 3, rows_of(j), :] * inv).astype(BF)
+        probs[w * HEADS + h, rows_of(j), 256 * c : 256 * (c + 1)] = p
+
+    def mix(t):
+        h, c = units[t]
+        p = probs[w * HEADS + h, :, 256 * c : 256 * (c + 1)]
+        mixed[t] = nn(vt[HD * h : HD * (h + 1)], p)
+
+    heads = [only_head(qt, h) for h in range(HEADS)]
+    n, steps = len(units), TOK // 64
+    for t in range(-1, n + 1):
+        if 0 <= t < n:
+            m = jnp.max(top[t], axis=0, keepdims=True)
+        if t >= 1:
+            inv = 1.0 / jnp.sum(sums[t - 1], axis=0, keepdims=True)
+        for j in range(steps):
+            if t + 1 < n:
+                score(t + 1, j)
+            if 0 <= t < n:
+                power(t, j, m)
+            if t >= 1:
+                weigh(t - 1, j, inv)
+        if t >= 1:
+            mix(t - 1)
+    out = [jnp.concatenate([mixed[2 * h], mixed[2 * h + 1]], axis=1) for h in range(HEADS)]
+    return jnp.concatenate(out, axis=0)
+
+
+def attn_backward(w, qt, kt, vn, dmix, delta, probs, dbuf, ebuf):
+    units = [(h, k, c) for h in range(HEADS) for c in range(2) for k in range(2)]
+    dq, dk, dv = {}, {}, {}
+    heads = [only_head(dmix, h) for h in range(HEADS)]
+
+    def tile(i):
+        return slice(256 * i, 256 * (i + 1))
+
+    def grow(table, key, v):
+        table[key] = v if key not in table else table[key] + v
+
+    def first(t, j):
+        h, k, c = units[t]
+        rows = slice(256 * k + 128 * j, 256 * k + 128 * (j + 1))
+        dbuf[t % 2, 128 * j : 128 * (j + 1), :] = nn(vn[rows], heads[h][:, tile(c)])
+
+    def middle(t, j):
+        h, k, c = units[t]
+        rows = slice(256 * k + 128 * j, 256 * k + 128 * (j + 1))
+        p = probs[w * HEADS + h, rows, tile(c)].astype(F32)
+        dp = dbuf[t % 2, 128 * j : 128 * (j + 1), :]
+        ds = p * (dp - delta[h : h + 1, tile(c)]) * SCALE
+        ebuf[t % 2, 128 * j : 128 * (j + 1), :] = ds.astype(BF)
+
+    def last(t, j):
+        h, k, c = units[t]
+        rows = slice(HD * h, HD * (h + 1))
+        ds = ebuf[t % 2]
+        if j == 0:
+            grow(dq, (h, c), nn(kt[rows, tile(k)], ds))
+        elif j == 1:
+            grow(dk, (h, k), nt(qt[rows, tile(c)], ds))
+        elif j == 2:
+            grow(dv, (h, k), nt(dmix[rows, tile(c)], probs[w * HEADS + h, tile(k), tile(c)]))
+
+    n = len(units)
+    for t in range(-1, n + 1):
+        for j in range(max(256 // 128, 3)):
+            if t + 1 < n and j < 256 // 128:
+                first(t + 1, j)
+            if t >= 1:
+                last(t - 1, j)
+            if 0 <= t < n and j < 256 // 128:
+                middle(t, j)
+    parts = [jnp.concatenate([v[h, 0], v[h, 1]], axis=1) for v in (dq, dk, dv) for h in range(HEADS)]
+    return jnp.concatenate(parts, axis=0).astype(BF)
+
+
+def mlp_middle(h2, gb, wet, wr, acts, dus, ubuf):
+    blocks = [(r, c) for c in range(TOK // 256) for r in range(HID // 64)]
+
+    def box(t):
+        r, c = blocks[t]
+        return slice(64 * r, 64 * (r + 1)), slice(256 * c, 256 * (c + 1))
+
+    def first(t):
+        rows, cols = box(t)
+        ubuf[t % 2, 0] = nn(wet[rows, :], h2[:, cols])
+        ubuf[t % 2, 1] = nn(wr[rows, :], gb[:, cols])
+
+    def second(t):
+        rows, cols = box(t)
+        u = ubuf[t % 2, 0]
+        u2 = u * u
+        v = u * (GC + (GC * 0.044715) * u2)
+        th = jnp.tanh(v)
+        cdf = 0.5 + 0.5 * th
+        acts[rows, cols] = (u * cdf).astype(BF)
+        slope = cdf + (0.5 - 0.5 * (th * th)) * (u * (GC + (3 * 0.044715 * GC) * u2))
+        dus[rows, cols] = (ubuf[t % 2, 1] * slope).astype(BF)
+
+    for t in range(-1, len(blocks)):
+        if t + 1 < len(blocks):
+            first(t + 1)
+        if t >= 0:
+            second(t)
+
+
 def kernel(
     factor, tok_ref, up_ref, gain1_ref, gain2_ref, wa, wp, we, wrt,
     out_ref, o_one, o_two, o_attn, o_proj, o_exp, o_red,
-    rx, rg, ob, wat, wpt, wet, wr, gain1, gain2,
+    rx, rg, rb, ob, wat, wpt, wet, wr, gain1, gain2,
     s_red, s_exp, s_proj, s_two, s_attn, s_one,
-    probs, packed, vnat, h1s, n1s, r1s, mixes, dy1s, dmixs, deltas,
+    probs, packed, vnat, h1s, n1s, r1s, mixes, dy1s, dmixs, deltas, sbuf, dbuf, ebuf, acts, dus, ubuf,
     a_parts, a_got, a_cross, a_final, b_parts, b_got, b_cross, b_final,
-    x_send, x_recv, g_send, g_recv, x_own, g_own, y_send, y_recv, y_own, a_sems, b_sems,
+    x_send, x_recv, g_send, g_recv, x_own, g_own, y_send, y_recv, y_own, z_send, z_recv, a_sems, b_sems,
 ):
     a, b, first, second = place()
     barrier = pltpu.get_barrier_semaphore()
@@ -223,6 +375,12 @@
                 barrier, inc=1, device_id=neighbour(sign * dx, sign * dy), device_id_type=MESH
             )
 
+    for dx, dy in RELAYS:
+        for sign in (-1, 1):
+            pl.semaphore_signal(
+                barrier, inc=1, device_id=neighbour(sign * dx, sign * dy), device_id_type=MESH
+            )
+
     def greet(r, carry):
         pl.semaphore_signal(
             barrier, inc=1, device_id=device(lax.rem(first + r, GROUP), second), device_id_type=MESH
@@ -233,16 +391,36 @@
         return carry
 
     lax.fori_loop(1, GROUP, greet, 0)
-    for part in range(3):
+    for part in range(PARTS):
         own_in(tok_ref, rx, x_own, part).start()
         own_in(up_ref, rg, g_own, part).start()
-    pl.semaphore_wait(barrier, 2 * len(SHIFTS) + 2 * (GROUP - 1))
-    for part in range(3):
+    pl.semaphore_wait(barrier, 2 * len(SHIFTS) + 2 * len(RELAYS) + 2 * (GROUP - 1))
+    for part in range(PARTS):
         for k in range(3):
             halo_in(tok_ref, rx, x_send, x_recv, part, k).start()
-    for part in range(3):
-        for k in range(3):
-            halo_in(up_ref, rg, g_send, g_recv, part, k).start()
+    edge = lax.rem(b, 4) == 0
+    relay = lax.rem(b, 4) == RELAY_AT
+    for part in range(PARTS):
+        halo_in(up_ref, rg, g_send, g_recv, part, 2).start()
+
+    @pl.when(jnp.logical_not(edge))
+    def _():
+        for part in range(PARTS):
+            for k in range(2):
+                halo_in(up_ref, rg, g_send, g_recv, part, k).start()
+
+    @pl.when(edge)
+    def _():
+        for part in range(PARTS):
+            for k in range(2):
+                relay_in(up_ref, rb, g_send, z_recv, part, k).start()
+
+    def forward(part):
+        @pl.when(relay)
+        def _():
+            for k in range(2):
+                relay_in(up_ref, rb, g_send, z_recv, part, k).wait_recv()
+                relay_on(rb, rg, z_send, g_recv, part, k).start()
 
     wat[...] = flip(wa[...])
     wpt[...] = flip(wp[...])
@@ -258,7 +436,13 @@
     s_one[...] = jnp.zeros_like(s_one)
 
     def attend(w, carry):
-        for part in range(3):
+        for part in range(PARTS):
+
+            @pl.when(w == FORWARD[part])
+            def _(part=part):
+                forward(part)
+
+        for part in range(PARTS):
 
             @pl.when(w == READY[part])
             def _(part=part):
@@ -278,28 +462,14 @@
         qt, vt = pk[0:96], pk[192:288]
         kn = pk[96:192].T
         vnat[w] = vt.T
-        mixed = []
-        for h in range(HEADS):
-            qm = only_head(qt, h)
-            parts = []
-            for c in range(2):
-                cols = slice(256 * c, 256 * (c + 1))
-                s = nn(kn, qm[:, cols])
-                m = jnp.max(s, axis=0, keepdims=True)
-                e = jnp.exp2((s - m) * (SCALE * LOG2E))
-                inv = 1.0 / jnp.sum(e, axis=0, keepdims=True)
-                p = (e * inv).astype(BF)
-                probs[w * HEADS + h, :, cols] = p
-                parts.append(nn(vt[HD * h : HD * (h + 1)], p))
-            mixed.append(jnp.concatenate(parts, axis=1))
-        mixed_f = jnp.concatenate(mixed, axis=0)
+        mixed_f = attn_forward(w, qt, kn, vt, probs, sbuf)
         mixes[w] = mixed_f
         return carry
 
     lax.fori_loop(0, 8, attend, 0)
 
     def mlp(w, carry):
-        for part in range(3):
+        for part in range(PARTS):
 
             @pl.when(w == READY[part])
             def _(part=part):
@@ -316,16 +486,11 @@
         gain_b = wide(gain2[...])
         h2f, n2, r2 = norm_cols(y1, gain_b)
         h2 = h2f.astype(BF)
-        u = nn(wet[...], h2)
-        u2 = u * u
-        t = jnp.tanh(u * (GC + (GC * 0.044715) * u2))
-        cdf = 0.5 + 0.5 * t
-        act = (u * cdf).astype(BF)
-        slope = cdf + (0.5 * u) * (1.0 - t * t) * (GC + (3 * 0.044715 * GC) * u2)
         gf = load_window(rg, lo, hi)
         gb = gf.astype(BF)
-        s_red[...] += nt(gb, act)
-        du = (nn(wr[...], gb) * slope).astype(BF)
+        mlp_middle(h2, gb, wet, wr, acts, dus, ubuf)
+        s_red[...] += nt(gb, acts[...])
+        du = dus[...]
         s_exp[...] += nt(h2, du)
         dh2 = nn(we[...], du)
         s_two[...] += fold(dh2 * n2)
@@ -372,23 +537,7 @@
         vn = vnat[w]
         dmix = dmixs[w]
         delta = deltas[w]
-        dqs, dks, dvs = [], [], []
-        for h in range(HEADS):
-            rows = slice(HD * h, HD * (h + 1))
-            dm = only_head(dmix, h)
-            dq, dk, dv = [], 0.0, 0.0
-            for c in range(2):
-                cols = slice(256 * c, 256 * (c + 1))
-                p = probs[w * HEADS + h, :, cols]
-                dp = nn(vn, dm[:, cols])
-                ds = (p.astype(F32) * (dp - delta[h : h + 1, cols]) * SCALE).astype(BF)
-                dq.append(nn(kt[rows], ds))
-                dk = dk + nt(qt[rows, cols], ds)
-                dv = dv + nt(dmix[rows, cols], p)
-            dqs.append(jnp.concatenate(dq, axis=1))
-            dks.append(dk)
-            dvs.append(dv)
-        dpk = jnp.concatenate(dqs + dks + dvs, axis=0).astype(BF)
+        dpk = attn_backward(w, qt, kt, vn, dmix, delta, probs, dbuf, ebuf)
         s_attn[...] += nt(h1s[w], dpk)
         dh1 = nn(wa[...], dpk).astype(BF).astype(F32)
         n1 = n1s[w]
@@ -399,13 +548,17 @@
 
     lax.fori_loop(0, 8, back, 0)
 
-    one = jnp.broadcast_to(jnp.sum(s_one[...], axis=1, keepdims=True), (D, 96))
-    last = jnp.concatenate([s_attn[:, 256:288], one], axis=1)
-    tiles = [s_attn[:, 0:128], s_attn[:, 128:256], last]
-    for j in range(4):
-        for i in range(4):
-            rows = slice(ROWS_B * i, ROWS_B * (i + 1))
-            b_parts[4 * j + i] = tiles[j][rows] if j < 3 else jnp.zeros((ROWS_B, 128), F32)
+    for j in range(2):
+        for i in range(6):
+            b_parts[6 * j + i] = s_attn[16 * i : 16 * i + 16, 128 * j : 128 * j + 128]
+    rest = s_attn[:, 256:288]
+    rest = jnp.concatenate([rest[24 * i : 24 * i + 24] for i in range(4)], axis=1)
+    one = jnp.broadcast_to(jnp.sum(s_one[...], axis=1, keepdims=True), (D, 128)).T[0:8]
+    rest = jnp.concatenate([rest, jnp.concatenate([one, jnp.zeros((8, 32), F32)], axis=1)], axis=0)
+    b_parts[12] = rest[0:16]
+    b_parts[13] = rest[16:32]
+    for i in range(14, GROUP):
+        b_parts[i] = jnp.zeros((ROWS_B, 128), F32)
     reduce_start(b_parts, b_got, b_sems)
     for start in (15 * CH, 0):
         send_out(ob, out_ref, y_send, y_recv, y_own, pl.ds(start, CH))
@@ -417,10 +570,17 @@
     o_proj[...] = fa[6][:, 0:96]
     o_two[...] = fa[6].T[96:97]
     reduce_last(b_cross, b_final, b_sems)
-    for part in range(3):
+    for part in range(PARTS):
         for k in range(3):
             halo_in(tok_ref, rx, x_send, x_recv, part, k).wait_send()
             halo_in(up_ref, rg, g_send, g_recv, part, k).wait_send()
+
+    @pl.when(relay)
+    def _():
+        for part in range(PARTS):
+            for k in range(2):
+                relay_on(rb, rg, z_send, g_recv, part, k).wait_send()
+
     everything = pl.ds(0, 16 * CH)
     own_out(ob, out_ref, y_own, everything).wait()
     for k in range(3):
@@ -428,9 +588,11 @@
         done.wait_send()
         done.wait_recv()
     reduce_end(b_final, b_sems)
-    fb = [jnp.concatenate([b_final[4 * j + i] for i in range(4)], axis=0) for j in range(3)]
-    o_attn[...] = jnp.concatenate([fb[0], fb[1], fb[2][:, 0:32]], axis=1)
-    o_one[...] = fb[2].T[32:33]
+    fb = [jnp.concatenate([b_final[6 * j + i] for i in range(6)], axis=0) for j in range(2)]
+    rest = jnp.concatenate([b_final[12], b_final[13]], axis=0)
+    last = jnp.concatenate([rest[0:24, 32 * i : 32 * i + 32] for i in range(4)], axis=0)
+    o_attn[...] = jnp.concatenate(fb + [last], axis=1)
+    o_one[...] = rest[24:25, 0:96]
 
 
 def local(tokens, upstream, gain_one, gain_two, attn_weight, proj_weight, expand_weight, reduce_weight):
@@ -454,6 +616,7 @@
             shape((D, HID), F32),
         ],
         scratch_shapes=[
+            pltpu.VMEM((8, 8, 6144), BF),
             pltpu.VMEM((8, 8, 6144), BF),
             pltpu.VMEM((8, 8, 6144), BF),
             pltpu.VMEM((8, 8, 6144), BF),
@@ -479,13 +642,19 @@
             pltpu.VMEM((8, D, TOK), F32),
             pltpu.VMEM((8, D, TOK), BF),
             pltpu.VMEM((8, 8, TOK), F32),
+            pltpu.VMEM((3, TOK, 256), F32),
+            pltpu.VMEM((2, 256, 256), F32),
+            pltpu.VMEM((2, 256, 256), BF),
+            pltpu.VMEM((HID, TOK), BF),
+            pltpu.VMEM((HID, TOK), BF),
+            pltpu.VMEM((2, 2, 64, 256), F32),
         ]
         + [pltpu.VMEM((GROUP, ROWS_A, 128), F32)] * 4
         + [pltpu.VMEM((GROUP, ROWS_B, 128), F32)] * 4
-        + [dma((3, 3))] * 4
+        + [dma((PARTS, 3))] * 4
+        + [dma((PARTS,))] * 2
         + [dma((3,))] * 2
-        + [dma((3,))] * 2
-        + [dma, dma((2, 3)), dma((2, 3))],
+        + [dma, dma((PARTS, 3)), dma((PARTS, 3)), dma((2, 3)), dma((2, 3))],
         compiler_params=pltpu.CompilerParams(
             vmem_limit_bytes=56 * 1024 * 1024, collective_id=0, has_side_effects=True
         ),

time: 125 us -> 116 us (0.928)
  Pallas kernels: 118 us -> 108 us
    pallas_call x1, Pallas kernels: 118 us -> 108 us  [local(): pl.pallas_call(functools.partial(kernel, factor), in_specs=[hbm, hbm] + [...]
where the time goes in v3:
time: 116 us; the launch traced here: 115 us
  Pallas kernels  108 us (93%)
  local copies, waits for them, and re-layouts  6.23 us (5%)
    pallas_call x1, Pallas kernels, local(): pl.pallas_call(functools.partial(kernel, factor), in_specs=[hbm, hbm] + [...  108 us
    unnamed x19, local copies, waits for them, and re-layouts  6.23 us

profile of v3, /device:TPU:1, one launch (start us, length us, event | category | flops | bytes accessed | tf_op | source)
XLA Modules:
  0.0 115.4 jit_solution(7648385176246990587)
XLA Ops:
  0.6 108.5 %block_backward.1 = (bf16[8,8,6144]{2,1,0:T(8,128)(2,1)}, f32[1,96]{1,0:T(1,128)}, f32[1,96]{1,0:T(1,128)}, f32[96,288]{1,0:T(8,128)}, f32[96,96]{1,0:T(8,128)}, /*index=5*/f32[96,384]{1,0:T(8,128)}, f32[96,384]{1,0:T(8,128)}) custom-call(bf16[8,8,6144]{2,1,0:T(8,128)(2,1)} %tok_ref.1, bf16[8,8,6144]{2,1,0:T(8,128)(2,1)} %up_ref.1, f32[1,96]{1,0:T(1,128)} %bitcast.8, ...), custom_call_target="tpu_custom_call" | custom-call | tf_op jit(solution)/shard_map/block_backward/pallas_call | solution.py:605
  109.1 0.0 copy-start.5
  109.1 0.0 copy-start.2
  109.1 2.1 %copy.22 = bf16[8,8,6144]{2,1,0:T(8,128)(2,1)} copy(bf16[8,8,6144]{2,1,0:T(8,128)(2,1)} %get-tuple-element.28) | data formatting | bytes 1572864
  111.2 0.0 copy-done.5
  111.3 0.0 copy-start.4
  111.3 0.5 copy.23
  111.8 0.1 copy-done.4
  111.8 0.5 copy.24
  112.3 0.0 copy-done.2
  112.3 0.0 copy-start.3
  112.3 0.0 copy-start.1
  112.3 0.7 copy.25
  113.0 0.1 copy-done.3
  113.1 0.6 copy.26
  113.8 0.0 copy-done.1
  113.8 0.0 copy-start
  113.8 0.7 copy.27
  114.4 0.3 copy-done
  114.7 0.7 copy.28
Async XLA Ops:
  109.1 2.1 %copy-start.5 = (f32[1,96]{1,0:T(1,128)S(1)}, f32[1,96]{1,0:T(1,128)}, u32[]{:S(2)}) copy-start(f32[1,96]{1,0:T(1,128)} %get-tuple-element.15) | copy-start | bytes 1156
  109.1 3.2 %copy-start.2 = (f32[96,288]{1,0:T(8,128)S(1)}, f32[96,288]{1,0:T(8,128)}, u32[]{:S(2)}) copy-start(f32[96,288]{1,0:T(8,128)} %get-tuple-element.31) | copy-start | bytes 331780
  111.3 0.6 copy-start.4
  112.3 0.8 copy-start.3
  112.3 1.4 %copy-start.1 = (f32[96,384]{1,0:T(8,128)S(1)}, f32[96,384]{1,0:T(8,128)}, u32[]{:S(2)}) copy-start(f32[96,384]{1,0:T(8,128)} %get-tuple-element.33) | copy-start | bytes 442372
  113.8 1.0 copy-start

commit v4 on v3

--- a/solution.py
+++ b/solution.py
@@ -88,13 +88,15 @@
 NGX, NGY = 32, 8
 GROUP = 16
 SHIFTS = ((1, 1), (0, 1), (1, 0))
-RELAYS = ((0, 3), (0, 4), (1, 4), (1, -3))
+RELAYS = ((1, -3), (0, 4))
 CUTS = (0, 3 * CH, 7 * CH, 13 * CH, 16 * CH)
 PARTS = 4
 READY = (0, 1, 3, 6)
-FORWARD = (0, 1, 2, 3)
+FORWARD = (
+    (0, 0, True), (1, 1, True), (2, 2, True), (3, 3, True),
+    (3, 0, False), (4, 1, False), (5, 2, False), (6, 3, False),
+)
 ROWS_A, ROWS_B = 48, 16
-RELAY_STEP, RELAY_NEXT, RELAY_AT = 3, 4, 3
 
 
 def half(flag):
@@ -132,22 +134,34 @@
     )
 
 
-def relay_in(src, dst, send, recv, part, k):
-    dx, dy = SHIFTS[k]
+def relay_in(src, dst, send, recv, part):
     cols = pl.ds(CUTS[part], CUTS[part + 1] - CUTS[part])
-    a, b = neighbour(-dx, RELAY_STEP)
     return remote(
-        src.at[half(not dx), half(not dy), cols], dst.at[half(dx), half(dy), cols],
-        send.at[part, k], recv.at[part, k], (a, b),
-    )
-
-
-def relay_on(src, dst, send, recv, part, k):
-    dx, dy = SHIFTS[k]
-    cols = pl.ds(CUTS[part], CUTS[part + 1] - CUTS[part])
-    box = (half(dx), half(dy), cols)
+        src.at[half(0), half(0), cols], dst.at[half(1), half(1), cols],
+        send.at[part, 0], recv.at[part], neighbour(-1, 3),
+    )
+
+
+def relay_on(src, dst, send, recv, part):
+    box = (half(1), half(1), pl.ds(CUTS[part], CUTS[part + 1] - CUTS[part]))
+    return remote(src.at[box], dst.at[box], send.at[part], recv.at[part, 0], neighbour(0, 4))
+
+
+def piece(i):
+    if i < 7:
+        return pl.ds((2 * i + 1) * CH, 2 * CH)
+    return pl.ds(15 * CH if i == 7 else 0, CH)
+
+
+def relay_out(src, dst, send, recv, cols, i):
+    box = (half(1), half(1), cols)
+    return remote(src.at[box], dst.at[box], send.at[0], recv.at[i], neighbour(1, -3))
+
+
+def relay_done(src, dst, send, recv, cols):
     return remote(
-        src.at[box], dst.at[box], send.at[part, k], recv.at[part, k], neighbour(0, RELAY_NEXT)
+        src.at[half(1), half(1), cols], dst.at[half(0), half(0), cols],
+        send, recv.at[0], neighbour(0, 4),
     )
 
 
@@ -172,8 +186,18 @@
     )
 
 
-def send_out(src, dst, send, recv, sem, cols):
-    for k in range(3):
+def send_out(src, dst, send, recv, sem, via, via_recv, cols, i):
+    edge = lax.rem(lax.axis_index("gy"), 4) == 3
+
+    @pl.when(edge)
+    def _():
+        relay_out(src, via, send, via_recv, cols, i).start()
+
+    @pl.when(jnp.logical_not(edge))
+    def _():
+        halo_out(src, dst, send, recv, 0, cols).start()
+
+    for k in (1, 2):
         halo_out(src, dst, send, recv, k, cols).start()
     own_out(src, dst, sem, cols).start()
 
@@ -361,11 +385,11 @@
 def kernel(
     factor, tok_ref, up_ref, gain1_ref, gain2_ref, wa, wp, we, wrt,
     out_ref, o_one, o_two, o_attn, o_proj, o_exp, o_red,
-    rx, rg, rb, ob, wat, wpt, wet, wr, gain1, gain2,
+    rx, rg, rbx, rbg, rbo, ob, wat, wpt, wet, wr, gain1, gain2,
     s_red, s_exp, s_proj, s_two, s_attn, s_one,
     probs, packed, vnat, h1s, n1s, r1s, mixes, dy1s, dmixs, deltas, sbuf, dbuf, ebuf, acts, dus, ubuf,
     a_parts, a_got, a_cross, a_final, b_parts, b_got, b_cross, b_final,
-    x_send, x_recv, g_send, g_recv, x_own, g_own, y_send, y_recv, y_own, z_send, z_recv, a_sems, b_sems,
+    x_send, x_recv, g_send, g_recv, x_own, g_own, y_send, y_recv, y_own, zx_send, zx_recv, zg_send, zg_recv, zo_send, zo_recv, a_sems, b_sems,
 ):
     a, b, first, second = place()
     barrier = pltpu.get_barrier_semaphore()
@@ -394,34 +418,6 @@
     for part in range(PARTS):
         own_in(tok_ref, rx, x_own, part).start()
         own_in(up_ref, rg, g_own, part).start()
-    pl.semaphore_wait(barrier, 2 * len(SHIFTS) + 2 * len(RELAYS) + 2 * (GROUP - 1))
-    for part in range(PARTS):
-        for k in range(3):
-            halo_in(tok_ref, rx, x_send, x_recv, part, k).start()
-    edge = lax.rem(b, 4) == 0
-    relay = lax.rem(b, 4) == RELAY_AT
-    for part in range(PARTS):
-        halo_in(up_ref, rg, g_send, g_recv, part, 2).start()
-
-    @pl.when(jnp.logical_not(edge))
-    def _():
-        for part in range(PARTS):
-            for k in range(2):
-                halo_in(up_ref, rg, g_send, g_recv, part, k).start()
-
-    @pl.when(edge)
-    def _():
-        for part in range(PARTS):
-            for k in range(2):
-                relay_in(up_ref, rb, g_send, z_recv, part, k).start()
-
-    def forward(part):
-        @pl.when(relay)
-        def _():
-            for k in range(2):
-                relay_in(up_ref, rb, g_send, z_recv, part, k).wait_recv()
-                relay_on(rb, rg, z_send, g_recv, part, k).start()
-
     wat[...] = flip(wa[...])
     wpt[...] = flip(wp[...])
     wet[...] = flip(we[...])
@@ -435,12 +431,42 @@
     s_attn[...] = jnp.zeros_like(s_attn)
     s_one[...] = jnp.zeros_like(s_one)
 
+    pl.semaphore_wait(barrier, 2 * len(SHIFTS) + 2 * len(RELAYS) + 2 * (GROUP - 1))
+    edge = lax.rem(b, 4) == 0
+    relay = lax.rem(b, 4) == 3
+    for src, dst, via, send, recv, via_recv in (
+        (tok_ref, rx, rbx, x_send, x_recv, zx_recv),
+        (up_ref, rg, rbg, g_send, g_recv, zg_recv),
+    ):
+        for part in range(PARTS):
+
+            @pl.when(edge)
+            def _():
+                relay_in(src, via, send, via_recv, part).start()
+
+            @pl.when(jnp.logical_not(edge))
+            def _():
+                halo_in(src, dst, send, recv, part, 0).start()
+
+            for k in (1, 2):
+                halo_in(src, dst, send, recv, part, k).start()
+
+    def forward(part, first_array):
+        @pl.when(relay)
+        def _():
+            if first_array:
+                relay_in(tok_ref, rbx, x_send, zx_recv, part).wait_recv()
+                relay_on(rbx, rx, zx_send, x_recv, part).start()
+            else:
+                relay_in(up_ref, rbg, g_send, zg_recv, part).wait_recv()
+                relay_on(rbg, rg, zg_send, g_recv, part).start()
+
     def attend(w, carry):
-        for part in range(PARTS):
-
-            @pl.when(w == FORWARD[part])
-            def _(part=part):
-                forward(part)
+        for at, part, first_array in FORWARD:
+
+            @pl.when(w == at)
+            def _(part=part, first_array=first_array):
+                forward(part, first_array)
 
         for part in range(PARTS):
 
@@ -517,19 +543,29 @@
             a_parts[2 * j + i] = tiles[j][rows] if j < 7 else jnp.zeros((ROWS_A, 128), F32)
     reduce_start(a_parts, a_got, a_sems)
 
+    relay_back = lax.rem(b, 4) == 0
+
+    def pass_on(i):
+        @pl.when(relay_back)
+        def _():
+            relay_out(ob, rbo, y_send, zo_recv, piece(i), i).wait_recv()
+            relay_done(rbo, out_ref, zo_send, y_recv, piece(i)).start()
+
     def back(w, carry):
         @pl.when(w > 0)
         def _():
             cols = pl.ds(pl.multiple_of((2 * w - 1) * CH, 128), 2 * CH)
-            send_out(ob, out_ref, y_send, y_recv, y_own, cols)
-
-        @pl.when(w == 3)
+            send_out(ob, out_ref, y_send, y_recv, y_own, rbo, zo_recv, cols, w - 1)
+
+        @pl.when(jnp.logical_and(w > 2, relay_back))
+        def _():
+            cols = pl.ds(pl.multiple_of((2 * w - 5) * CH, 128), 2 * CH)
+            relay_out(ob, rbo, y_send, zo_recv, cols, w - 3).wait_recv()
+            relay_done(rbo, out_ref, zo_send, y_recv, cols).start()
+
+        @pl.when(w == 6)
         def _():
             reduce_middle(a_got, a_cross, a_sems, factor)
-
-        @pl.when(w == 6)
-        def _():
-            reduce_last(a_cross, a_final, a_sems)
 
         lo, hi = offsets(w)
         pk = packed[w]
@@ -560,8 +596,13 @@
     for i in range(14, GROUP):
         b_parts[i] = jnp.zeros((ROWS_B, 128), F32)
     reduce_start(b_parts, b_got, b_sems)
-    for start in (15 * CH, 0):
-        send_out(ob, out_ref, y_send, y_recv, y_own, pl.ds(start, CH))
+    for i in (7, 8):
+        send_out(ob, out_ref, y_send, y_recv, y_own, rbo, zo_recv, piece(i), i)
+    pass_on(5)
+    pass_on(6)
+    reduce_last(a_cross, a_final, a_sems)
+    pass_on(7)
+    pass_on(8)
     reduce_middle(b_got, b_cross, b_sems, factor)
     reduce_end(a_final, a_sems)
     fa = [jnp.concatenate([a_final[2 * j], a_final[2 * j + 1]], axis=0) for j in range(7)]
@@ -575,13 +616,18 @@
             halo_in(tok_ref, rx, x_send, x_recv, part, k).wait_send()
             halo_in(up_ref, rg, g_send, g_recv, part, k).wait_send()
 
+    everything = pl.ds(0, 16 * CH)
+
     @pl.when(relay)
     def _():
         for part in range(PARTS):
-            for k in range(2):
-                relay_on(rb, rg, z_send, g_recv, part, k).wait_send()
-
-    everything = pl.ds(0, 16 * CH)
+            relay_on(rbx, rx, zx_send, x_recv, part).wait_send()
+            relay_on(rbg, rg, zg_send, g_recv, part).wait_send()
+
+    @pl.when(relay_back)
+    def _():
+        relay_done(rbo, out_ref, zo_send, y_recv, everything).wait_send()
+
     own_out(ob, out_ref, y_own, everything).wait()
     for k in range(3):
         done = halo_out(ob, out_ref, y_send, y_recv, k, everything)
@@ -593,6 +639,11 @@
     last = jnp.concatenate([rest[0:24, 32 * i : 32 * i + 32] for i in range(4)], axis=0)
     o_attn[...] = jnp.concatenate(fb + [last], axis=1)
     o_one[...] = rest[24:25, 0:96]
+
+
+def finish(*refs):
+    for src, dst in zip(refs[:7], refs[7:]):
+        dst[...] = src[...]
 
 
 def local(tokens, upstream, gain_one, gain_two, attn_weight, proj_weight, expand_weight, reduce_weight):
@@ -616,6 +667,8 @@
             shape((D, HID), F32),
         ],
         scratch_shapes=[
+            pltpu.VMEM((8, 8, 6144), BF),
+            pltpu.VMEM((8, 8, 6144), BF),
             pltpu.VMEM((8, 8, 6144), BF),
             pltpu.VMEM((8, 8, 6144), BF),
             pltpu.VMEM((8, 8, 6144), BF),
@@ -654,7 +707,9 @@
         + [dma((PARTS, 3))] * 4
         + [dma((PARTS,))] * 2
         + [dma((3,))] * 2
-        + [dma, dma((PARTS, 3)), dma((PARTS, 3)), dma((2, 3)), dma((2, 3))],
+        + [dma]
+        + [dma((PARTS,))] * 4
+        + [dma, dma((9,)), dma((2, 3)), dma((2, 3))],
         compiler_params=pltpu.CompilerParams(
             vmem_limit_bytes=56 * 1024 * 1024, collective_id=0, has_side_effects=True
         ),
@@ -663,7 +718,13 @@
         tokens, upstream, gain_one.reshape(1, D), gain_two.reshape(1, D),
         attn_weight, proj_weight, expand_weight, reduce_weight.T,
     )
-    grad, one, two, attn, proj, exp, red = outs
+    grad, one, two, attn, proj, exp, red = pl.pallas_call(
+        finish,
+        in_specs=[vm] * 7,
+        out_specs=[vm] * 7,
+        out_shape=[shape(v.shape, v.dtype) for v in outs],
+        name="finish",
+    )(*outs)
     return (grad, one.reshape(D), two.reshape(D), attn, proj, exp, red.T)
 
 

time: 116 us -> 108 us (0.931)
  local copies, waits for them, and re-layouts: 6.23 us -> 0 us
    unnamed x19 -> x0, local copies, waits for them, and re-layouts: 6.23 us -> none
    pallas_call x1, Pallas kernels: 108 us -> 105 us  [local(): pl.pallas_call(functools.partial(kernel, factor), in_specs=[hbm, hbm] + [...]
    pallas_call x0 -> x1, Pallas kernels: none -> 2.37 us  [local(): pl.pallas_call(finish, in_specs=[vm] * 7, out_specs=[vm] * 7, out_shape=[...]
where the time goes in v4:
time: 108 us
  Pallas kernels  107 us (99%)
    pallas_call x1, Pallas kernels, local(): pl.pallas_call(functools.partial(kernel, factor), in_specs=[hbm, hbm] + [...  105 us
    pallas_call x1, Pallas kernels, local(): pl.pallas_call(finish, in_specs=[vm] * 7, out_specs=[vm] * 7, out_shape=[...  2.37 us

profile of v4, /device:TPU:1, one launch (start us, length us, event | category | flops | bytes accessed | tf_op | source)
XLA Modules:
  0.0 107.6 jit_solution(3945749252450616573)
XLA Ops:
  0.6 104.6 %block_backward.1 = (bf16[8,8,6144]{2,1,0:T(8,128)(2,1)}, f32[1,96]{1,0:T(1,128)}, f32[1,96]{1,0:T(1,128)}, f32[96,288]{1,0:T(8,128)}, f32[96,96]{1,0:T(8,128)}, /*index=5*/f32[96,384]{1,0:T(8,128)}, f32[96,384]{1,0:T(8,128)}) custom-call(bf16[8,8,6144]{2,1,0:T(8,128)(2,1)} %tok_ref.1, bf16[8,8,6144]{2,1,0:T(8,128)(2,1)} %up_ref.1, f32[1,96]{1,0:T(1,128)} %bitcast.7, ...), custom_call_target="tpu_custom_call" | custom-call | tf_op jit(solution)/shard_map/block_backward/pallas_call | solution.py:656
  105.2 2.4 %finish.1 = (bf16[8,8,6144]{2,1,0:T(8,128)(2,1)}, f32[1,96]{1,0:T(1,128)}, f32[1,96]{1,0:T(1,128)}, f32[96,288]{1,0:T(8,128)}, f32[96,96]{1,0:T(8,128)}, /*index=5*/f32[96,384]{1,0:T(8,128)}, f32[96,384]{1,0:T(8,128)}) custom-call(bf16[8,8,6144]{2,1,0:T(8,128)(2,1)} %get-tuple-element.21.refs_0_, f32[1,96]{1,0:T(1,128)} %get-tuple-element.22.refs_1_, ...), custom_call_target="tpu_custom_call" | custom-call | tf_op jit(solution)/shard_map/finish/pallas_call | solution.py:721

commit v5 on v4

--- a/solution.py
+++ b/solution.py
@@ -105,13 +105,13 @@
 
 def place():
     a, b = lax.axis_index("gx"), lax.axis_index("gy")
-    first = (b // 4) * 8 + lax.rem(a, 8)
-    second = (a // 8) * 4 + lax.rem(b, 4)
+    first = (a // 8) * 4 + lax.rem(b, 4)
+    second = (b // 4) * 8 + lax.rem(a, 8)
     return a, b, first, second
 
 
 def device(first, second):
-    return ((second // 4) * 8 + lax.rem(first, 8), (first // 8) * 4 + lax.rem(second, 4))
+    return ((first // 4) * 8 + lax.rem(second, 8), (second // 8) * 4 + lax.rem(first, 4))
 
 
 def neighbour(dx, dy):
@@ -305,7 +305,7 @@
 
 
 def attn_backward(w, qt, kt, vn, dmix, delta, probs, dbuf, ebuf):
-    units = [(h, k, c) for h in range(HEADS) for c in range(2) for k in range(2)]
+    units = [(h, k, c) for k in range(2) for h in range(HEADS) for c in range(2)]
     dq, dk, dv = {}, {}, {}
     heads = [only_head(dmix, h) for h in range(HEADS)]
 
@@ -563,7 +563,7 @@
             relay_out(ob, rbo, y_send, zo_recv, cols, w - 3).wait_recv()
             relay_done(rbo, out_ref, zo_send, y_recv, cols).start()
 
-        @pl.when(w == 6)
+        @pl.when(w == 5)
         def _():
             reduce_middle(a_got, a_cross, a_sems, factor)
 
@@ -598,19 +598,17 @@
     reduce_start(b_parts, b_got, b_sems)
     for i in (7, 8):
         send_out(ob, out_ref, y_send, y_recv, y_own, rbo, zo_recv, piece(i), i)
-    pass_on(5)
-    pass_on(6)
+    for i in (5, 6, 7, 8):
+        pass_on(i)
+    reduce_middle(b_got, b_cross, b_sems, factor)
     reduce_last(a_cross, a_final, a_sems)
-    pass_on(7)
-    pass_on(8)
-    reduce_middle(b_got, b_cross, b_sems, factor)
+    reduce_last(b_cross, b_final, b_sems)
     reduce_end(a_final, a_sems)
     fa = [jnp.concatenate([a_final[2 * j], a_final[2 * j + 1]], axis=0) for j in range(7)]
     o_red[...] = jnp.concatenate(fa[0:3], axis=1)
     o_exp[...] = jnp.concatenate(fa[3:6], axis=1)
     o_proj[...] = fa[6][:, 0:96]
     o_two[...] = fa[6].T[96:97]
-    reduce_last(b_cross, b_final, b_sems)
     for part in range(PARTS):
         for k in range(3):
             halo_in(tok_ref, rx, x_send, x_recv, part, k).wait_send()

time: 108 us -> 103 us (0.954)
  Pallas kernels: 107 us -> 102 us
    pallas_call x1, Pallas kernels: 105 us -> 99.4 us  [local(): pl.pallas_call(functools.partial(kernel, factor), in_specs=[hbm, hbm] + [...]
where the time goes in v5:
time: 103 us; the launch traced here: 102 us
  Pallas kernels  102 us (99%)
    pallas_call x1, Pallas kernels, local(): pl.pallas_call(functools.partial(kernel, factor), in_specs=[hbm, hbm] + [...  99.4 us
    pallas_call x1, Pallas kernels, local(): pl.pallas_call(finish, in_specs=[vm] * 7, out_specs=[vm] * 7, out_shape=[...  2.37 us

profile of v5, /device:TPU:1, one launch (start us, length us, event | category | flops | bytes accessed | tf_op | source)
XLA Modules:
  0.0 102.4 jit_solution(16255612725796975949)
XLA Ops:
  0.6 99.4 %block_backward.1 = (bf16[8,8,6144]{2,1,0:T(8,128)(2,1)}, f32[1,96]{1,0:T(1,128)}, f32[1,96]{1,0:T(1,128)}, f32[96,288]{1,0:T(8,128)}, f32[96,96]{1,0:T(8,128)}, /*index=5*/f32[96,384]{1,0:T(8,128)}, f32[96,384]{1,0:T(8,128)}) custom-call(bf16[8,8,6144]{2,1,0:T(8,128)(2,1)} %tok_ref.1, bf16[8,8,6144]{2,1,0:T(8,128)(2,1)} %up_ref.1, f32[1,96]{1,0:T(1,128)} %bitcast.7, ...), custom_call_target="tpu_custom_call" | custom-call | tf_op jit(solution)/shard_map/block_backward/pallas_call | solution.py:654
  100.1 2.4 %finish.1 = (bf16[8,8,6144]{2,1,0:T(8,128)(2,1)}, f32[1,96]{1,0:T(1,128)}, f32[1,96]{1,0:T(1,128)}, f32[96,288]{1,0:T(8,128)}, f32[96,96]{1,0:T(8,128)}, /*index=5*/f32[96,384]{1,0:T(8,128)}, f32[96,384]{1,0:T(8,128)}) custom-call(bf16[8,8,6144]{2,1,0:T(8,128)(2,1)} %get-tuple-element.21.refs_0_, f32[1,96]{1,0:T(1,128)} %get-tuple-element.22.refs_1_, ...), custom_call_target="tpu_custom_call" | custom-call | tf_op jit(solution)/shard_map/finish/pallas_call | solution.py:719

commit v6 on v5

--- a/solution.py
+++ b/solution.py
@@ -304,7 +304,7 @@
     return jnp.concatenate(out, axis=0)
 
 
-def attn_backward(w, qt, kt, vn, dmix, delta, probs, dbuf, ebuf):
+def attn_backward(w, qt, kt, vn, dmix, delta, probs, dbuf, ebuf, extra):
     units = [(h, k, c) for k in range(2) for h in range(HEADS) for c in range(2)]
     dq, dk, dv = {}, {}, {}
     heads = [only_head(dmix, h) for h in range(HEADS)]
@@ -348,6 +348,8 @@
                 last(t - 1, j)
             if 0 <= t < n and j < 256 // 128:
                 middle(t, j)
+        if t in extra:
+            extra[t]()
     parts = [jnp.concatenate([v[h, 0], v[h, 1]], axis=1) for v in (dq, dk, dv) for h in range(HEADS)]
     return jnp.concatenate(parts, axis=0).astype(BF)
 
@@ -387,7 +389,7 @@
     out_ref, o_one, o_two, o_attn, o_proj, o_exp, o_red,
     rx, rg, rbx, rbg, rbo, ob, wat, wpt, wet, wr, gain1, gain2,
     s_red, s_exp, s_proj, s_two, s_attn, s_one,
-    probs, packed, vnat, h1s, n1s, r1s, mixes, dy1s, dmixs, deltas, sbuf, dbuf, ebuf, acts, dus, ubuf,
+    probs, packed, vnat, h1s, n1s, r1s, mixes, dy1s, dmixs, deltas, dpks, sbuf, dbuf, ebuf, acts, dus, ubuf,
     a_parts, a_got, a_cross, a_final, b_parts, b_got, b_cross, b_final,
     x_send, x_recv, g_send, g_recv, x_own, g_own, y_send, y_recv, y_own, zx_send, zx_recv, zg_send, zg_recv, zo_send, zo_recv, a_sems, b_sems,
 ):
@@ -551,38 +553,56 @@
             relay_out(ob, rbo, y_send, zo_recv, piece(i), i).wait_recv()
             relay_done(rbo, out_ref, zo_send, y_recv, piece(i)).start()
 
+    def rest_of(v):
+        held = {}
+
+        def weights():
+            s_attn[...] += nt(h1s[v], dpks[...])
+
+        def product():
+            held[0] = nn(wa[...], dpks[...]).astype(BF).astype(F32)
+
+        def gains():
+            s_one[...] += fold(held[0] * n1s[v])
+
+        def result():
+            lo, hi = offsets(v)
+            part = norm_back(held[0], n1s[v], r1s[v][0:1], wide(gain1[...]))
+            store_window(ob, lo, hi, dy1s[v] + part)
+
+        return {0: weights, 2: product, 4: gains, 6: result}
+
+    dpks[...] = jnp.zeros_like(dpks)
+
     def back(w, carry):
-        @pl.when(w > 0)
+        @pl.when(w > 1)
         def _():
-            cols = pl.ds(pl.multiple_of((2 * w - 1) * CH, 128), 2 * CH)
-            send_out(ob, out_ref, y_send, y_recv, y_own, rbo, zo_recv, cols, w - 1)
-
-        @pl.when(jnp.logical_and(w > 2, relay_back))
+            cols = pl.ds(pl.multiple_of((2 * w - 3) * CH, 128), 2 * CH)
+            send_out(ob, out_ref, y_send, y_recv, y_own, rbo, zo_recv, cols, w - 2)
+
+        @pl.when(jnp.logical_and(w > 3, relay_back))
         def _():
-            cols = pl.ds(pl.multiple_of((2 * w - 5) * CH, 128), 2 * CH)
-            relay_out(ob, rbo, y_send, zo_recv, cols, w - 3).wait_recv()
+            cols = pl.ds(pl.multiple_of((2 * w - 7) * CH, 128), 2 * CH)
+            relay_out(ob, rbo, y_send, zo_recv, cols, w - 4).wait_recv()
             relay_done(rbo, out_ref, zo_send, y_recv, cols).start()
 
         @pl.when(w == 5)
         def _():
             reduce_middle(a_got, a_cross, a_sems, factor)
 
-        lo, hi = offsets(w)
         pk = packed[w]
-        qt, kt = pk[0:96], pk[96:192]
-        vn = vnat[w]
-        dmix = dmixs[w]
-        delta = deltas[w]
-        dpk = attn_backward(w, qt, kt, vn, dmix, delta, probs, dbuf, ebuf)
-        s_attn[...] += nt(h1s[w], dpk)
-        dh1 = nn(wa[...], dpk).astype(BF).astype(F32)
-        n1 = n1s[w]
-        s_one[...] += fold(dh1 * n1)
-        r1 = r1s[w][0:1]
-        store_window(ob, lo, hi, dy1s[w] + norm_back(dh1, n1, r1, wide(gain1[...])))
+        dpk = attn_backward(
+            w, pk[0:96], pk[96:192], vnat[w], dmixs[w], deltas[w], probs, dbuf, ebuf,
+            rest_of(lax.rem(w + 7, 8)),
+        )
+        dpks[...] = dpk
         return carry
 
     lax.fori_loop(0, 8, back, 0)
+    send_out(ob, out_ref, y_send, y_recv, y_own, rbo, zo_recv, piece(6), 6)
+    steps = rest_of(7)
+    for t in (0, 2, 4):
+        steps[t]()
 
     for j in range(2):
         for i in range(6):
@@ -596,9 +616,12 @@
     for i in range(14, GROUP):
         b_parts[i] = jnp.zeros((ROWS_B, 128), F32)
     reduce_start(b_parts, b_got, b_sems)
+    steps[6]()
+    for i in (4, 5):
+        pass_on(i)
     for i in (7, 8):
         send_out(ob, out_ref, y_send, y_recv, y_own, rbo, zo_recv, piece(i), i)
-    for i in (5, 6, 7, 8):
+    for i in (6, 7, 8):
         pass_on(i)
     reduce_middle(b_got, b_cross, b_sems, factor)
     reduce_last(a_cross, a_final, a_sems)
@@ -693,6 +716,7 @@
             pltpu.VMEM((8, D, TOK), F32),
             pltpu.VMEM((8, D, TOK), BF),
             pltpu.VMEM((8, 8, TOK), F32),
+            pltpu.VMEM((3 * D, TOK), BF),
             pltpu.VMEM((3, TOK, 256), F32),
             pltpu.VMEM((2, 256, 256), F32),
             pltpu.VMEM((2, 256, 256), BF),

time: 103 us -> 103 us (level)
  no operation moved by 1% of the time
where the time goes in v6:
time: 103 us
  Pallas kernels  103 us (100%)
    pallas_call x1, Pallas kernels, local(): pl.pallas_call(functools.partial(kernel, factor), in_specs=[hbm, hbm] + [...  100 us
    pallas_call x1, Pallas kernels, local(): pl.pallas_call(finish, in_specs=[vm] * 7, out_specs=[vm] * 7, out_shape=[...  2.37 us

profile of v6, /device:TPU:1, one launch (start us, length us, event | category | flops | bytes accessed | tf_op | source)
XLA Modules:
  0.0 103.2 jit_solution(6404216197954304536)
XLA Ops:
  0.6 100.1 %block_backward.1 = (bf16[8,8,6144]{2,1,0:T(8,128)(2,1)}, f32[1,96]{1,0:T(1,128)}, f32[1,96]{1,0:T(1,128)}, f32[96,288]{1,0:T(8,128)}, f32[96,96]{1,0:T(8,128)}, /*index=5*/f32[96,384]{1,0:T(8,128)}, f32[96,384]{1,0:T(8,128)}) custom-call(bf16[8,8,6144]{2,1,0:T(8,128)(2,1)} %tok_ref.1, bf16[8,8,6144]{2,1,0:T(8,128)(2,1)} %up_ref.1, f32[1,96]{1,0:T(1,128)} %bitcast.7, ...), custom_call_target="tpu_custom_call" | custom-call | tf_op jit(solution)/shard_map/block_backward/pallas_call | solution.py:677
  100.8 2.4 %finish.1 = (bf16[8,8,6144]{2,1,0:T(8,128)(2,1)}, f32[1,96]{1,0:T(1,128)}, f32[1,96]{1,0:T(1,128)}, f32[96,288]{1,0:T(8,128)}, f32[96,96]{1,0:T(8,128)}, /*index=5*/f32[96,384]{1,0:T(8,128)}, f32[96,384]{1,0:T(8,128)}) custom-call(bf16[8,8,6144]{2,1,0:T(8,128)(2,1)} %get-tuple-element.21.refs_0_, f32[1,96]{1,0:T(1,128)} %get-tuple-element.22.refs_1_, ...), custom_call_target="tpu_custom_call" | custom-call | tf_op jit(solution)/shard_map/finish/pallas_call | solution.py:743
